TPU v7x, 32 devices: a whole 2x2x4 slice. The times are simulated.
32 devices in a mesh: fsdp: 8 (over z, y), dp: 4 (over x, core).
Axes of the slice: x: 2, y: 2, z: 4, core: 2. Of those that a mesh axis runs over, the one named last changes fastest.
Arguments:
- tokens: bfloat16 [32, 512, 768], P(None, ('fsdp', 'dp')), may hold values from -6 to 6
- cotangent: bfloat16 [32, 512, 768], P(None, ('fsdp', 'dp')), may hold values from -6 to 6
- lengths: int32 [32], replicated, may hold values from 1 to 512, 10240 in all
- device_sequence: int32 [32], replicated, may hold values from 0 to 31, each once
- slot_device: int32 [32], replicated, may hold values from 0 to 31, each once
- attention_master: float32 [3072, 768], P(('fsdp', 'dp')), may hold values from -0.649519 to 0.649519
- feedforward_master: float32 [2048, 3, 768], P(('fsdp', 'dp')), may hold values from -0.26516504 to 0.26516504
- gains_master: float32 [2, 768], P(None, ('fsdp', 'dp')), may hold values from 0.5 to 1.5
- attention_mean: float32 [3072, 768], P(('fsdp', 'dp')), may hold values from -384 to 384
- attention_square: float32 [3072, 768], P(('fsdp', 'dp')), may hold values from 1024 to 16384
- feedforward_mean: float32 [2048, 3, 768], P(('fsdp', 'dp')), may hold values from -320 to 320
- feedforward_square: float32 [2048, 3, 768], P(('fsdp', 'dp')), may hold values from 655.36 to 10485.76
- gains_mean: float32 [2, 768], P(None, ('fsdp', 'dp')), may hold values from -1280 to 1280
- gains_square: float32 [2, 768], P(None, ('fsdp', 'dp')), may hold values from 9830.4 to 163840
Outputs:
- output: bfloat16 [32, 512, 768], P(None, ('fsdp', 'dp'))
- input_gradient: bfloat16 [32, 512, 768], P(None, ('fsdp', 'dp'))
- attention_gradient: float32 [3072, 768], P(('fsdp', 'dp'))
- feedforward_gradient: float32 [2048, 3, 768], P(('fsdp', 'dp'))
- gains_gradient: float32 [2, 768], P(None, ('fsdp', 'dp'))
- mean_attention: float32 [3072, 768], P(('fsdp', 'dp'))
- square_attention: float32 [3072, 768], P(('fsdp', 'dp'))
- mean_feedforward: float32 [2048, 3, 768], P(('fsdp', 'dp'))
- square_feedforward: float32 [2048, 3, 768], P(('fsdp', 'dp'))
- mean_gains: float32 [2, 768], P(None, ('fsdp', 'dp'))
- square_gains: float32 [2, 768], P(None, ('fsdp', 'dp'))
- master_attention: float32 [3072, 768], P(('fsdp', 'dp'))
- master_feedforward: float32 [2048, 3, 768], P(('fsdp', 'dp'))
- gains_update: float32 [2, 768], P(None, ('fsdp', 'dp'))
- copy_attention: bfloat16 [3072, 768], P(('fsdp', 'dp'))
- copy_feedforward: bfloat16 [2048, 3, 768], P(('fsdp', 'dp'))
Inputs may be any that keep to these rules, and one draw needn't show every extreme that they name: One sequence has exactly 512 tokens; the lengths sum to 10240. `device_sequence`: each sequence is dealt to exactly one device. `slot_device`: each device fills exactly one output slot.
All inputs are finite; a program needn't handle non-finite values.
Results may differ from a plain program's by a relative error of at most 0.02.
The roundings to bfloat16 on the way count: a program that leaves them out, or rounds other values in their place, can miss the bound.
Values may be sent and summed in bfloat16 or wider, within the bound.
A program may use at most 128 MiB of HBM per device.

v0:
```python
import jax
import jax.numpy as jnp
from jax import lax
from jax.sharding import PartitionSpec as P

H = 12
KVH = 12
HD = 64
STEP = 4


norm_epsilon = 1e-05
attn_multiplier = 0.125
residual_multiplier = 1.0
rope_theta = 10000.0
beta_first = 0.5
beta_second = 0.5
learning_rate = 0.03
weight_decay = 0.1
adam_epsilon = 1e-08


def rope_tables(length):
    half_width = HD // 2
    frequency = rope_theta ** (-(jnp.arange(half_width, dtype=jnp.float32) * 2.0) / HD)
    angles = jnp.arange(length, dtype=jnp.float32)[:, None] * frequency[None, :]
    return (jnp.cos(angles), jnp.sin(angles))


def rotate(values, cosine, sine_table):
    half_width = values.shape[-1] // 2
    first_half = values[..., :half_width]
    second_half = values[..., half_width:]
    cosine = cosine[:, None, :]
    sine_table = sine_table[:, None, :]
    return jnp.concatenate(
        [
            first_half * cosine - second_half * sine_table,
            second_half * cosine + first_half * sine_table,
        ],
        axis=-1,
    )


def rotate_back(gradient, cosine, sine_table):
    half_width = gradient.shape[-1] // 2
    first_half = gradient[..., :half_width]
    second_half = gradient[..., half_width:]
    cosine = cosine[:, None, :]
    sine_table = sine_table[:, None, :]
    return jnp.concatenate(
        [
            first_half * cosine + second_half * sine_table,
            second_half * cosine - first_half * sine_table,
        ],
        axis=-1,
    )


def times_rows(left, right):
    return lax.dot_general(
        left, right, (((1,), (1,)), ((), ())), preferred_element_type=jnp.float32
    )


def times_tokens(left, right):
    return lax.dot_general(
        left, right, (((0,), (0,)), ((), ())), preferred_element_type=jnp.float32
    )


def norm_reverse_pass(values, inverse, gradient, gain):
    scaled = gradient * gain
    return inverse * scaled - values * inverse * inverse * inverse * jnp.mean(
        values * scaled, axis=-1, keepdims=True
    )


def adam_update(master, gradient, first_moment, second_moment, decay):
    first_new = beta_first * first_moment + (1.0 - beta_first) * gradient
    second_new = beta_second * second_moment + (1.0 - beta_second) * gradient * gradient
    first_hat = first_new / (1.0 - beta_first**STEP)
    second_hat = second_new / (1.0 - beta_second**STEP)
    master_new = master - learning_rate * (
        first_hat / (jnp.sqrt(second_hat) + adam_epsilon) + decay * master
    )
    return (first_new, second_new, master_new)


def causal_block(start_row, block_rows, length):
    return (start_row + jnp.arange(block_rows))[:, None] >= jnp.arange(length)[None, :]


def block_scores(query_block, key_heads, causal):
    scores = (
        jnp.einsum("ikrh,jkh->krij", query_block, key_heads, preferred_element_type=jnp.float32)
        * attn_multiplier
    )
    return jnp.where(causal, scores, -1e30)


def local(
    tokens,
    cotangent,
    lengths,
    device_sequence,
    slot_device,
    attention_master,
    feedforward_master,
    gains_master,
    attention_mean,
    attention_square,
    feedforward_mean,
    feedforward_square,
    gains_mean,
    gains_square,
):
    devices = lax.axis_size(("fsdp", "dp"))
    own_index = lax.axis_index(("fsdp", "dp"))
    positions = tokens.shape[1]
    width = tokens.shape[2]
    length = positions * devices
    repeat = H // KVH
    query_key_value_rows = (H + 2 * KVH) * HD
    block_rows = min(512, length)
    counter = jnp.arange(devices, dtype=jnp.int32)
    slot_of_device = jnp.sum(
        jnp.where(slot_device[:, None] == counter[None, :], counter[:, None], 0), axis=0
    )
    slot_of_sequence = jnp.sum(
        jnp.where(device_sequence[:, None] == counter[None, :], counter[:, None], 0), axis=0
    )
    sent_tokens = jnp.take(tokens, device_sequence, axis=0)
    sent_cotangent = jnp.take(cotangent, slot_of_device, axis=0)
    got_tokens, received_cotangent = (
        lax.all_to_all(sent_tokens, ("fsdp", "dp"), split_axis=0, concat_axis=1, tiled=True),
        lax.all_to_all(sent_cotangent, ("fsdp", "dp"), split_axis=0, concat_axis=1, tiled=True),
    )
    seq_tokens = got_tokens.reshape(length, width).astype(jnp.float32)
    own_length = lengths[device_sequence[own_index]]
    valid = jnp.arange(length, dtype=jnp.int32) < own_length
    attention_low = attention_master.astype(jnp.bfloat16)
    feedforward_low = feedforward_master.astype(jnp.bfloat16)
    gains_low = gains_master.astype(jnp.bfloat16)
    attention_full, feedforward_full, gains_full = (
        lax.all_gather(attention_low, ("fsdp", "dp"), axis=0, tiled=True),
        lax.all_gather(feedforward_low, ("fsdp", "dp"), axis=0, tiled=True),
        lax.all_gather(gains_low, ("fsdp", "dp"), axis=1, tiled=True),
    )
    gain_one = gains_full[0].astype(jnp.float32)
    gain_two = gains_full[1].astype(jnp.float32)
    cosine, sine_table = rope_tables(length)
    inverse_one = lax.rsqrt(
        jnp.mean(seq_tokens * seq_tokens, axis=-1, keepdims=True) + norm_epsilon
    )
    normed_one = (seq_tokens * inverse_one * gain_one).astype(jnp.bfloat16)
    projected = times_rows(normed_one, attention_full[:query_key_value_rows])
    query_heads = (
        rotate(projected[:, : H * HD].reshape(length, H, HD), cosine, sine_table)
        .astype(jnp.bfloat16)
        .reshape(length, KVH, repeat, HD)
    )
    key_heads = rotate(
        projected[:, H * HD : (H + KVH) * HD].reshape(length, KVH, HD), cosine, sine_table
    ).astype(jnp.bfloat16)
    value_heads = projected[:, (H + KVH) * HD :].reshape(length, KVH, HD).astype(jnp.bfloat16)
    block_number = 0
    start_row = block_number * block_rows
    masked = block_scores(query_heads, key_heads, causal_block(start_row, block_rows, length))
    row_max = jnp.max(masked, axis=-1, keepdims=True)
    shifted_exp = jnp.exp(masked - row_max)
    denominator = jnp.sum(shifted_exp, axis=-1, keepdims=True)
    probabilities = (shifted_exp / denominator).astype(jnp.bfloat16)
    log_totals = [row_max + jnp.log(denominator)]
    combined_parts = jnp.einsum(
        "krij,jkh->ikrh", probabilities, value_heads, preferred_element_type=jnp.float32
    ).reshape(block_rows, H * HD)
    combined_heads = combined_parts.astype(jnp.bfloat16)
    branch_one = jnp.dot(
        combined_heads, attention_full[query_key_value_rows:], preferred_element_type=jnp.float32
    )
    hidden_state = seq_tokens + residual_multiplier * branch_one
    inverse_two = lax.rsqrt(
        jnp.mean(hidden_state * hidden_state, axis=-1, keepdims=True) + norm_epsilon
    )
    normed_two = (hidden_state * inverse_two * gain_two).astype(jnp.bfloat16)
    gate_values = times_rows(normed_two, feedforward_full[:, 0])
    up_values = times_rows(normed_two, feedforward_full[:, 1])
    sigmoid_values = jax.nn.sigmoid(gate_values)
    silu_values = gate_values * sigmoid_values
    activation = (silu_values * up_values).astype(jnp.bfloat16)
    branch_two = jnp.dot(activation, feedforward_full[:, 2], preferred_element_type=jnp.float32)
    result = hidden_state + residual_multiplier * branch_two
    output_rows = jnp.where(valid[:, None], result, 0.0).astype(jnp.bfloat16)
    attention_back, feedforward_back = (
        lax.all_gather(attention_low, ("fsdp", "dp"), axis=0, tiled=True),
        lax.all_gather(feedforward_low, ("fsdp", "dp"), axis=0, tiled=True),
    )
    cot_rows = jnp.where(
        valid[:, None], received_cotangent.reshape(length, width).astype(jnp.float32), 0.0
    )
    down_grad = (residual_multiplier * cot_rows).astype(jnp.bfloat16)
    act_grad = times_rows(down_grad, feedforward_back[:, 2])
    silu_slope = sigmoid_values * (1.0 + gate_values * (1.0 - sigmoid_values))
    gate_grad = (act_grad * up_values * silu_slope).astype(jnp.bfloat16)
    up_grad = (act_grad * silu_values).astype(jnp.bfloat16)
    normed_two_grad = jnp.dot(
        gate_grad, feedforward_back[:, 0], preferred_element_type=jnp.float32
    ) + jnp.dot(up_grad, feedforward_back[:, 1], preferred_element_type=jnp.float32)
    gain_two_grad = jnp.sum(hidden_state * inverse_two * normed_two_grad, axis=0)
    hidden_grad = cot_rows + norm_reverse_pass(hidden_state, inverse_two, normed_two_grad, gain_two)
    branch_grad = (residual_multiplier * hidden_grad).astype(jnp.bfloat16)
    mixed_grad = (
        times_rows(branch_grad, attention_back[query_key_value_rows:])
        .astype(jnp.bfloat16)
        .reshape(length, KVH, repeat, HD)
    )
    block_number = 0
    start_row = block_number * block_rows
    masked = block_scores(query_heads, key_heads, causal_block(start_row, block_rows, length))
    recomputed = jnp.exp(masked - log_totals[block_number])
    value_grad = jnp.einsum(
        "krij,ikrh->jkh",
        recomputed.astype(jnp.bfloat16),
        mixed_grad,
        preferred_element_type=jnp.float32,
    )
    prob_grad = jnp.einsum(
        "ikrh,jkh->krij", mixed_grad, value_heads, preferred_element_type=jnp.float32
    )
    score_grad = (
        recomputed * (prob_grad - jnp.sum(recomputed * prob_grad, axis=-1, keepdims=True))
    ).astype(jnp.bfloat16)
    query_parts = (
        jnp.einsum("krij,jkh->ikrh", score_grad, key_heads, preferred_element_type=jnp.float32)
        * attn_multiplier
    )
    key_grad = (
        jnp.einsum("krij,ikrh->jkh", score_grad, query_heads, preferred_element_type=jnp.float32)
        * attn_multiplier
    )
    projected_grad = jnp.concatenate(
        [
            rotate_back(query_parts.reshape(length, H, HD), cosine, sine_table).reshape(
                length, H * HD
            ),
            rotate_back(key_grad, cosine, sine_table).reshape(length, KVH * HD),
            value_grad.reshape(length, KVH * HD),
        ],
        axis=1,
    ).astype(jnp.bfloat16)
    normed_one_grad = jnp.dot(
        projected_grad, attention_back[:query_key_value_rows], preferred_element_type=jnp.float32
    )
    gain_one_grad = jnp.sum(seq_tokens * inverse_one * normed_one_grad, axis=0)
    input_rows = (
        hidden_grad + norm_reverse_pass(seq_tokens, inverse_one, normed_one_grad, gain_one)
    ).astype(jnp.bfloat16)
    attention_term = jnp.concatenate(
        [times_tokens(projected_grad, normed_one), times_tokens(combined_heads, branch_grad)],
        axis=0,
    )
    gains_term = jnp.stack([gain_one_grad, gain_two_grad], axis=0)
    attention_gradient, gains_gradient = (
        lax.psum_scatter(attention_term, ("fsdp", "dp"), scatter_dimension=0, tiled=True),
        lax.psum_scatter(gains_term, ("fsdp", "dp"), scatter_dimension=1, tiled=True),
    )
    feedforward_gradient = lax.psum_scatter(
        jnp.stack(
            [
                times_tokens(gate_grad, normed_two),
                times_tokens(up_grad, normed_two),
                times_tokens(activation, down_grad),
            ],
            axis=1,
        ),
        ("fsdp", "dp"),
        scatter_dimension=0,
        tiled=True,
    )
    back_output, back_input = (
        lax.all_to_all(
            output_rows.reshape(1, length, width),
            ("fsdp", "dp"),
            split_axis=1,
            concat_axis=0,
            tiled=True,
        ),
        lax.all_to_all(
            input_rows.reshape(1, length, width),
            ("fsdp", "dp"),
            split_axis=1,
            concat_axis=0,
            tiled=True,
        ),
    )
    output = jnp.take(back_output, slot_device, axis=0)
    input_gradient = jnp.take(back_input, slot_of_sequence, axis=0)
    mean_attention, square_attention, master_attention = adam_update(
        attention_master, attention_gradient, attention_mean, attention_square, weight_decay
    )
    mean_feedforward, square_feedforward, master_feedforward = adam_update(
        feedforward_master, feedforward_gradient, feedforward_mean, feedforward_square, weight_decay
    )
    mean_gains, square_gains, master_gains = adam_update(
        gains_master, gains_gradient, gains_mean, gains_square, 0.0
    )
    gains_update = master_gains - gains_master
    return (
        output,
        input_gradient,
        attention_gradient,
        feedforward_gradient,
        gains_gradient,
        mean_attention,
        square_attention,
        mean_feedforward,
        square_feedforward,
        mean_gains,
        square_gains,
        master_attention,
        master_feedforward,
        gains_update,
        master_attention.astype(jnp.bfloat16),
        master_feedforward.astype(jnp.bfloat16),
    )


def solution(mesh):
    in_specs = (
        P(None, ("fsdp", "dp"), None),
        P(None, ("fsdp", "dp"), None),
        P(),
        P(),
        P(),
        P(("fsdp", "dp"), None),
        P(("fsdp", "dp"), None, None),
        P(None, ("fsdp", "dp")),
        P(("fsdp", "dp"), None),
        P(("fsdp", "dp"), None),
        P(("fsdp", "dp"), None, None),
        P(("fsdp", "dp"), None, None),
        P(None, ("fsdp", "dp")),
        P(None, ("fsdp", "dp")),
    )
    out_specs = (
        P(None, ("fsdp", "dp"), None),
        P(None, ("fsdp", "dp"), None),
        P(("fsdp", "dp"), None),
        P(("fsdp", "dp"), None, None),
        P(None, ("fsdp", "dp")),
        P(("fsdp", "dp"), None),
        P(("fsdp", "dp"), None),
        P(("fsdp", "dp"), None, None),
        P(("fsdp", "dp"), None, None),
        P(None, ("fsdp", "dp")),
        P(None, ("fsdp", "dp")),
        P(("fsdp", "dp"), None),
        P(("fsdp", "dp"), None, None),
        P(None, ("fsdp", "dp")),
        P(("fsdp", "dp"), None),
        P(("fsdp", "dp"), None, None),
    )
    return jax.shard_map(local, mesh=mesh, in_specs=in_specs, out_specs=out_specs, check_vma=False)
```

profile of v0, /device:TPU:8, one launch (start us, length us, event | category | flops | bytes accessed | tf_op | source)
XLA Modules:
  0.0 608.7 jit_solution(6652986261299240789)
XLA Ops:
  9.0 1.8 convert_element_type.119
  13.2 6.0 all-to-all-start
  21.1 21.6 %all-to-all-done = bf16[32,16,768]{2,1,0:T(8,128)(2,1)S(1)} async-done(((bf16[32,16,768]{2,1,0:T(8,128)(2,1)}), bf16[32,16,768]{2,1,0:T(8,128)(2,1)S(1)}, u32[]{:S(2)}, u32[]{:S(2)}) %all-to-all-start) | async-done | bytes 786464 | tf_op jit(solution)/shard_map/all_to_all | solution.py:136
  42.7 4.0 all-to-all-start.2
  48.6 51.3 %all-gather = bf16[32,24,2]{1,2,0:T(2,128)(2,1)S(1)} all-gather(bf16[1,24,2]{1,2,0:T(2,128)(2,1)S(1)} %convert_bitcast_fusion), channel_id=1, replica_groups=mesh['fsdp'=8,'dp'=4] {'fsdp','dp'}, dimensions={0}, use_global_device_ids=true | all-gather | bytes 3168 | tf_op jit(solution)/shard_map/all_gather | solution.py:148
  107.5 4.0 fusion.15
  111.5 2.1 copy-done.4
  114.9 3.8 fusion.67
  118.6 1.9 copy.75
  120.5 3.1 copy.76
  123.6 2.0 subtract_convert_fusion.3
  125.6 2.2 fusion.68
  127.9 1.9 fusion.3
  129.7 2.7 copy-done.2
  132.4 2.6 fusion.40
  135.1 2.8 multiply_reduce_fusion.2
  139.6 28.6 %all-gather.6.cloned.1.call-done = bf16[2048,3,768]{2,0,1:T(8,128)(2,1)} async-done(((bf16[64,3,768]{2,0,1:T(8,128)(2,1)}), bf16[2048,3,768]{2,0,1:T(8,128)(2,1)}) %all-gather.6.cloned.1.call-update) | async-done | bytes 9437200 | tf_op jit(solution)/shard_map/all_gather | solution.py:147
  168.2 4.1 fusion.18
  172.3 3.8 fusion.20
  176.2 4.8 multiply_convert_fusion
  183.1 2.5 multiply_reduce_fusion
  185.6 3.0 fusion.35
  188.6 3.0 convolution_convert_fusion
  193.0 6.8 %fusion.37 = bf16[12,64,512]{2,1,0:T(8,128)(2,1)S(1)} fusion(bf16[512,12,64]{0,2,1:T(8,128)(2,1)S(1)} %bitcast.160, f32[12,1,512,512]{2,3,0,1:T(8,128)} %copy-done.2, f32[12,512]{1,0:T(8,128)} %log_add_fusion), kind=kOutput, calls=%fused_computation.75 | convolution fusion | flops 409337856 | bytes 14180352 | tf_op jit(solution)/shard_map/krij,ikrh->jkh/dot_general | solution.py:222
  199.8 9.2 %fusion = (f32[12,512]{1,0:T(8,128)S(1)}, f32[12,512,512]{2,1,0:T(8,128)}) fusion(f32[12,1,512,512]{2,3,0,1:T(8,128)} %copy-done.2, f32[12,512]{1,0:T(8,128)S(1)} %copy-done.30, bf16[512,12,64]{0,2,1:T(8,128)(2,1)S(1)} %bitcast.169, bf16[512,12,64]{0,2,1:T(8,128)(2,1)S(1)} %bitcast.161), kind=kOutput, calls=%fused_computation.8 | convolution fusion | flops 412084224 | bytes 26787840 | tf_op jit(solution)/shard_map/ikrh,jkh->krij/dot_general | solution.py:228
  209.1 7.1 %fusion.8 = bf16[12,512,512]{1,2,0:T(8,128)(2,1)S(1)} fusion(f32[12,512,512]{2,1,0:T(8,128)} %get-tuple-element.62, f32[12,1,512,512]{2,3,0,1:T(8,128)S(1)} %bitcast.159, f32[12,512]{1,0:T(8,128)S(1)} %get-tuple-element.61, f32[12,512]{1,0:T(8,128)S(1)} %copy-done.30), kind=kLoop, calls=%fused_computation.19 | loop fusion | flops 12582912 | bytes 31506432 | tf_op jit(solution)/shard_map/reshape.33
  217.3 2.0 multiply_bitcast_fusion
  219.4 2.2 fusion.48
  223.5 4.9 fusion.46
  228.3 7.9 %pad_maximum_fusion.1 = f32[3072,768]{1,0:T(8,128)} fusion(f32[768,768]{1,0:T(8,128)} %fusion.48, f32[2304,768]{1,0:T(8,128)} %fusion.46), kind=kLoop, calls=%fused_computation.16 | loop fusion | flops 2359296 | bytes 18874368 | tf_op jit(solution)/shard_map/concatenate | solution.py:259
  237.4 3.6 convolution_bitcast_fusion.1
  241.0 1.9 convolution_bitcast_fusion.2
  242.9 1.9 convolution_bitcast_fusion
  244.8 7.4 %pad_maximum_fusion = f32[2048,3,768]{2,0,1:T(8,128)} fusion(f32[2048,1,768]{2,0,1:T(8,128)S(1)} %convolution_bitcast_fusion, f32[2048,1,768]{2,0,1:T(8,128)S(1)} %convolution_bitcast_fusion.1, f32[2048,1,768]{2,0,1:T(8,128)S(1)} %convolution_bitcast_fusion.2), kind=kLoop, calls=%fused_computation.4 | loop fusion | flops 9437184 | bytes 37748736 | tf_op jit(solution)/shard_map/stack | solution.py:269
  252.9 5.1 fusion.43
  258.0 2.4 copy.95
  260.9 6.5 %reduce.11 = bf16[512,768]{1,0:T(8,128)(2,1)S(1)} reduce(bf16[512,1,768]{2,1,0:T(2,128)(2,1)} %bitcast.162, bf16[]{:T(256)} %broadcast.205), dimensions={1}, to_apply=%bitcast.157.reduce_sub_computation | reduce | bytes 1572866
  268.4 4.0 all-to-all-start.1
  272.4 5.3 fusion.32
  279.6 5.5 reduce.12
  286.1 10.8 %all-to-all-done.1 = bf16[32,2,6144]{2,1,0:T(2,128)(2,1)S(1)} async-done(((bf16[32,2,6144]{2,1,0:T(2,128)(2,1)}), bf16[32,2,6144]{2,1,0:T(2,128)(2,1)S(1)}, u32[]{:S(2)}, u32[]{:S(2)}) %all-to-all-start.1) | async-done | bytes 786464 | tf_op jit(solution)/shard_map/all_to_all | solution.py:282
  296.9 7.5 %all-to-all-start.3 = ((bf16[32,2,6144]{2,1,0:T(2,128)(2,1)}), bf16[32,2,6144]{2,1,0:T(2,128)(2,1)S(1)}, u32[]{:S(2)}, u32[]{:S(2)}) async-start(bf16[32,2,6144]{2,1,0:T(2,128)(2,1)} %reshape.322), calls=%async_computation.3 | async-start | bytes 1572864 | tf_op jit(solution)/shard_map/all_to_all | solution.py:289
  304.6 48.8 %all-reduce = f32[2,768]{1,0:T(2,128)S(1)} all-reduce(f32[2,768]{1,0:T(2,128)S(1)} %pad_maximum_fusion.13), channel_id=4, replica_groups=mesh['fsdp'=8,'dp'=4] {'fsdp','dp'}, use_global_device_ids=true, to_apply=%region_13.15.clone | all-reduce | flops 1536 | bytes 12288
  357.4 1.8 gather_fusion.3
  361.3 26.0 %reduce-scatter.4.cloned.1.call-done = f32[96,768]{1,0:T(8,128)} async-done(((f32[3072,768]{1,0:T(8,128)}), f32[96,768]{1,0:T(8,128)}) %reduce-scatter.4.cloned.1.call-update) | async-done | bytes 294928 | tf_op jit(solution)/shard_map/reduce_scatter | solution.py:265
  387.3 2.2 fusion.64
  389.5 209.3 %reduce-scatter.6.cloned.1.call-done = f32[64,3,768]{2,0,1:T(8,128)} async-done(((f32[2048,3,768]{2,0,1:T(8,128)}), f32[64,3,768]{2,0,1:T(8,128)}) %reduce-scatter.6.cloned.1.call-update) | async-done | bytes 589840 | tf_op jit(solution)/shard_map/reduce_scatter | solution.py:268
  598.8 2.9 fusion.62
  (184 shorter events, 35.2 us)
Async XLA Ops:
  7.2 4.4 copy-start
  7.2 5.0 copy-start.41
  7.2 99.4 %all-gather.4.cloned.1.call-start = ((), (), s32[]{:S(2)}) async-start(), calls=%async_computation.6 | async-start | bytes 4866048 | tf_op jit(solution)/shard_map/all_gather | solution.py:146
  9.0 159.2 %all-gather.6.cloned.1.call-start = ((), (), s32[]{:S(2)}) async-start(), calls=%async_computation.7 | async-start | bytes 9732096 | tf_op jit(solution)/shard_map/all_gather | solution.py:147
  11.5 7.7 %copy-start.43 = (s32[32]{0:T(128)S(1)}, s32[32]{0:T(128)}, u32[]{:S(2)}) copy-start(s32[32]{0:T(128)} %param.20) | copy-start | bytes 388
  11.5 7.8 %copy-start.19 = (bf16[32,16,768]{2,1,0:T(8,128)(2,1)S(1)}, bf16[32,16,768]{2,1,0:T(8,128)(2,1)}, u32[]{:S(2)}) copy-start(bf16[32,16,768]{2,1,0:T(8,128)(2,1)} %param.17) | copy-start | bytes 2359300
  13.2 29.4 %all-to-all-start = ((bf16[32,16,768]{2,1,0:T(8,128)(2,1)}), bf16[32,16,768]{2,1,0:T(8,128)(2,1)S(1)}, u32[]{:S(2)}, u32[]{:S(2)}) async-start(bf16[32,16,768]{2,1,0:T(8,128)(2,1)} %broadcast_select_fusion.3), calls=%async_computation | async-start | bytes 1572864 | tf_op jit(solution)/shard_map/all_to_all | solution.py:136
  19.4 29.2 %copy-start.34 = (f32[2,24]{1,0:T(2,128)S(1)}, f32[2,24]{1,0:T(2,128)}, u32[]{:S(2)}) copy-start(f32[2,24]{1,0:T(2,128)} %param.23) | copy-start | bytes 580
  19.4 81.3 %copy-start.40 = (s32[32]{0:T(128)S(1)}, s32[32]{0:T(128)}, u32[]{:S(2)}) copy-start(s32[32]{0:T(128)} %param.18) | copy-start | bytes 388
  42.7 62.6 %all-to-all-start.2 = ((bf16[32,16,768]{2,1,0:T(8,128)(2,1)}), bf16[32,16,768]{2,1,0:T(8,128)(2,1)S(1)}, u32[]{:S(2)}, u32[]{:S(2)}) async-start(bf16[32,16,768]{2,1,0:T(8,128)(2,1)} %broadcast_select_fusion.1), calls=%async_computation.2 | async-start | bytes 1572864 | tf_op jit(solution)/shard_map/all_to_all | solution.py:137
  46.7 340.6 %reduce-scatter.4.cloned.1.call-start = ((), (), s32[]{:S(2)}) async-start(), calls=%async_computation.8 | async-start | bytes 9732096 | tf_op jit(solution)/shard_map/reduce_scatter | solution.py:265
  125.6 2.3 copy-start.8
  125.6 2.2 copy-start.10
  127.8 4.6 copy-start.2
  127.9 4.6 copy-start.5
  135.1 2.8 copy-start.17
  137.8 45.0 %copy-start.3 = (f32[512,768]{1,0:T(8,128)}, f32[512,768]{1,0:T(8,128)S(1)}, u32[]{:S(2)}) copy-start(f32[512,768]{1,0:T(8,128)S(1)} %get-tuple-element.59) | copy-start | bytes 4718596
  168.2 4.1 copy-start.23
  168.2 8.0 %slice-start.3 = ((s8[9437184]{0:T(1024)(128)(4,1)}), s8[4194304]{0:T(1024)(128)(4,1)S(1)}, s32[]{:S(2)}) async-start(s8[9437184]{0:T(1024)(128)(4,1)} %bitcast.183), calls=%async_computation.13 | async-start | bytes 8388608
  168.2 8.0 %slice-start.4 = ((s8[9437184]{0:T(1024)(128)(4,1)}), s8[4194304]{0:T(1024)(128)(4,1)S(1)}, s32[]{:S(2)}) async-start(s8[9437184]{0:T(1024)(128)(4,1)} %bitcast.183), calls=%async_computation.14 | async-start | bytes 8388608
  172.3 3.9 copy-start.22
  172.3 3.9 slice-start.5
  183.1 2.5 copy-start.38
  193.0 6.8 %copy-start.6 = (bf16[512,768]{0,1:T(8,128)(2,1)S(1)}, bf16[512,768]{0,1:T(8,128)(2,1)}, u32[]{:S(2)}) copy-start(bf16[512,768]{0,1:T(8,128)(2,1)} %copy.74) | copy-start | bytes 2359300
  193.0 6.8 %copy-start.30 = (f32[12,512]{1,0:T(8,128)S(1)}, f32[12,512]{1,0:T(8,128)}, u32[]{:S(2)}) copy-start(f32[12,512]{1,0:T(8,128)} %log_add_fusion) | copy-start | bytes 73732
  193.0 16.0 %slice-start = ((s8[12582912]{0:T(1024)(128)(4,1)}), s8[4194304]{0:T(1024)(128)(4,1)S(1)}, s32[]{:S(2)}) async-start(s8[12582912]{0:T(1024)(128)(4,1)} %bitcast.158), calls=%async_computation.10 | async-start | bytes 8388608
  193.0 16.0 %slice-start.1 = ((s8[12582912]{0:T(1024)(128)(4,1)}), s8[4194304]{0:T(1024)(128)(4,1)S(1)}, s32[]{:S(2)}) async-start(s8[12582912]{0:T(1024)(128)(4,1)} %bitcast.158), calls=%async_computation.11 | async-start | bytes 8388608
  199.8 22.4 %copy-start.15 = (bf16[12,64,512]{2,1,0:T(8,128)(2,1)}, bf16[12,64,512]{2,1,0:T(8,128)(2,1)S(1)}, u32[]{:S(2)}) copy-start(bf16[12,64,512]{2,1,0:T(8,128)(2,1)S(1)} %fusion.37) | copy-start | bytes 2359300
  199.8 9.2 %slice-start.2 = ((s8[12582912]{0:T(1024)(128)(4,1)}), s8[4194304]{0:T(1024)(128)(4,1)S(1)}, s32[]{:S(2)}) async-start(s8[12582912]{0:T(1024)(128)(4,1)} %bitcast.158), calls=%async_computation.12 | async-start | bytes 8388608
  209.1 7.1 %copy-start.11 = (bf16[512,12,32]{0,2,1:T(8,128)(2,1)S(1)}, bf16[512,12,32]{0,2,1:T(8,128)(2,1)}, u32[]{:S(2)}) copy-start(bf16[512,12,32]{0,2,1:T(8,128)(2,1)} %copy-done.10) | copy-start | bytes 1179652
  209.1 7.1 %copy-start.13 = (bf16[512,12,32]{0,2,1:T(8,128)(2,1)S(1)}, bf16[512,12,32]{0,2,1:T(8,128)(2,1)}, u32[]{:S(2)}) copy-start(bf16[512,12,32]{0,2,1:T(8,128)(2,1)} %copy-done.12) | copy-start | bytes 1179652
  219.3 2.3 copy-start.27
  219.3 2.2 copy-start.28
  236.3 362.6 %reduce-scatter.6.cloned.1.call-start = ((), (), s32[]{:S(2)}) async-start(), calls=%async_computation.9 | async-start | bytes 19464192 | tf_op jit(solution)/shard_map/reduce_scatter | solution.py:268
  237.4 3.6 copy-start.47
  268.4 28.5 %all-to-all-start.1 = ((bf16[32,2,6144]{2,1,0:T(2,128)(2,1)}), bf16[32,2,6144]{2,1,0:T(2,128)(2,1)S(1)}, u32[]{:S(2)}, u32[]{:S(2)}) async-start(bf16[32,2,6144]{2,1,0:T(2,128)(2,1)} %reshape.320), calls=%async_computation.1 | async-start | bytes 1572864 | tf_op jit(solution)/shard_map/all_to_all | solution.py:282
  279.5 24.9 %copy-start.44 = (s32[32]{0:T(128)S(1)}, s32[32]{0:T(128)}, u32[]{:S(2)}) copy-start(s32[32]{0:T(128)} %param.20) | copy-start | bytes 388
  279.5 24.9 %copy-start.42 = (s32[32]{0:T(128)S(1)}, s32[32]{0:T(128)}, u32[]{:S(2)}) copy-start(s32[32]{0:T(128)} %param.19) | copy-start | bytes 388
  279.5 25.1 %copy-start.33 = (f32[768]{0:T(1024)S(1)}, f32[768]{0:T(1024)}, u32[]{:S(2)}) copy-start(f32[768]{0:T(1024)} %get-tuple-element.17) | copy-start | bytes 9220
  279.5 73.9 %copy-start.35 = (f32[2,24]{1,0:T(2,128)S(1)}, f32[2,24]{1,0:T(2,128)}, u32[]{:S(2)}) copy-start(f32[2,24]{1,0:T(2,128)} %param.23) | copy-start | bytes 580
  279.6 73.9 %copy-start.36 = (f32[2,24]{1,0:T(2,128)S(1)}, f32[2,24]{1,0:T(2,128)}, u32[]{:S(2)}) copy-start(f32[2,24]{1,0:T(2,128)} %param.29) | copy-start | bytes 580
  279.6 73.9 %copy-start.37 = (f32[2,24]{1,0:T(2,128)S(1)}, f32[2,24]{1,0:T(2,128)}, u32[]{:S(2)}) copy-start(f32[2,24]{1,0:T(2,128)} %param.28) | copy-start | bytes 580
  296.9 58.1 %all-to-all-start.3 = ((bf16[32,2,6144]{2,1,0:T(2,128)(2,1)}), bf16[32,2,6144]{2,1,0:T(2,128)(2,1)S(1)}, u32[]{:S(2)}, u32[]{:S(2)}) async-start(bf16[32,2,6144]{2,1,0:T(2,128)(2,1)} %reshape.322), calls=%async_computation.3 | async-start | bytes 1572864 | tf_op jit(solution)/shard_map/all_to_all | solution.py:289
  357.4 29.9 %copy-start.14 = (f32[96,768]{1,0:T(8,128)S(1)}, f32[96,768]{1,0:T(8,128)}, u32[]{:S(2)}) copy-start(f32[96,768]{1,0:T(8,128)} %param.21) | copy-start | bytes 884740
  357.4 29.9 %copy-start.31 = (f32[96,768]{1,0:T(8,128)S(1)}, f32[96,768]{1,0:T(8,128)}, u32[]{:S(2)}) copy-start(f32[96,768]{1,0:T(8,128)} %param.25) | copy-start | bytes 884740
  359.2 239.6 %copy-start.7 = (f32[64,3,768]{2,0,1:T(8,128)S(1)}, f32[64,3,768]{2,0,1:T(8,128)}, u32[]{:S(2)}) copy-start(f32[64,3,768]{2,0,1:T(8,128)} %param.22) | copy-start | bytes 1769476
  359.2 239.6 %copy-start.29 = (f32[64,3,768]{2,0,1:T(8,128)S(1)}, f32[64,3,768]{2,0,1:T(8,128)}, u32[]{:S(2)}) copy-start(f32[64,3,768]{2,0,1:T(8,128)} %param.27) | copy-start | bytes 1769476
  387.3 214.4 %copy-start.1 = (bf16[32,16,768]{2,1,0:T(8,128)(2,1)S(1)}, bf16[32,16,768]{2,1,0:T(8,128)(2,1)}, u32[]{:S(2)}) copy-start(bf16[32,16,768]{2,1,0:T(8,128)(2,1)} %param.16) | copy-start | bytes 2359300
  (15 other events, 23.4 us)
Sparse Core Ops, SparseCore 0:
  11.5 72.2 all-gather.3
  87.2 80.9 all-gather.5
  236.4 150.8 reduce-scatter.3
  395.3 203.5 reduce-scatter.5
where the time goes:
time: 620 us; the launch traced here: 609 us
  waiting for transfers between devices  296 us (48%)
  blocking collectives  100 us (16%)
  matrix products  75.5 us (12%)
  other arithmetic  63.5 us (10%)
  local copies, waits for them, and re-layouts  34.3 us (6%)
  starting transfers between devices  21.6 us (3%)
  between operations  17.3 us (3%)
    reduce_scatter x1, waiting for transfers between devices, local(): lax.psum_scatter(jnp.stack([times_tokens(gate_grad, normed_two), times_to...  209 us
    all_gather x1, blocking collectives, local(): lax.all_gather(gains_low, ('fsdp', 'dp'), axis=1, tiled=True)  51.3 us
    unnamed x1, blocking collectives  48.8 us
    all_gather x1, waiting for transfers between devices, local(): lax.all_gather(feedforward_low, ('fsdp', 'dp'), axis=0, tiled=True)  28.6 us
    reduce_scatter x1, waiting for transfers between devices, local(): lax.psum_scatter(attention_term, ('fsdp', 'dp'), scatter_dimension=0, til...  26 us
    all_to_all x1, waiting for transfers between devices, local(): lax.all_to_all(sent_tokens, ('fsdp', 'dp'), split_axis=0, concat_axis=1,...  21.6 us
    dot_general x5, matrix products, times_rows(): lax.dot_general(left, right, (((1,), (1,)), ((), ())), preferred_element_...  19.7 us
    unnamed x118, local copies, waits for them, and re-layouts  14.5 us
  transfers between devices with their start and end apart: 8, of which 5 were waited for; matrix products, arithmetic and copies ran while one was open for 15% of the time, Pallas kernels for 0%

commit v1 on v0

v1 whole, which is shorter than its diff:
```python
import functools
import jax, jax.numpy as jnp, numpy as np
from jax import lax
from jax.experimental import pallas as pl
from jax.experimental.pallas import tpu as pltpu
H=12; KVH=12; HD=64; STEP=4
norm_epsilon=1e-05; attn_multiplier=0.125; rope_theta=10000.0
f32=jnp.float32; bf16=jnp.bfloat16
LOG2E=1.4426950408889634

def dot_nt(a,b):
    return lax.dot_general(a,b,(((1,),(1,)),((),())),preferred_element_type=f32)
def dot_nn(a,b):
    return lax.dot_general(a,b,(((1,),(0,)),((),())),preferred_element_type=f32)
def dot_tn(a,b):
    return lax.dot_general(a,b,(((0,),(0,)),((),())),preferred_element_type=f32)

def tables(length):
    half=HD//2
    freq=(np.float32(rope_theta)**(-(np.arange(half,dtype=np.float32)*np.float32(2.0))/np.float32(HD))).astype(np.float32)
    ang=(np.arange(length,dtype=np.float32)[:,None]*freq[None,:]).astype(np.float32)
    c=np.cos(ang.astype(np.float64)).astype(np.float32); s=np.sin(ang.astype(np.float64)).astype(np.float32)
    C=np.concatenate([c,c,c,c],1); S=np.concatenate([-s,s,-s,s],1)
    return C,S

RB=64
def rows_loop(length, body):
    def it(i,carry):
        body(pl.ds(pl.multiple_of(i*RB,RB),RB), i*RB)
        return carry
    lax.fori_loop(0,length//RB,it,0)

def norm_block(xv, gain):
    inv=lax.rsqrt(jnp.mean(xv*xv,axis=-1,keepdims=True)+norm_epsilon)
    return inv

def swap_halves(x):
    lane=lax.broadcasted_iota(jnp.int32,x.shape,1)
    return jnp.where(lax.rem(lane,64)<32, pltpu.roll(x,96,1), pltpu.roll(x,32,1))

def phase_norm1(x_ref,g_ref,n1_ref):
    L=x_ref.shape[0]
    def body(r,_):
        xv=x_ref[r,:].astype(f32)
        inv=norm_block(xv,None)
        n1_ref[r,:]=(xv*inv*g_ref[0:1,:]).astype(bf16)
    rows_loop(L,body)

def phase_qkv(n1_ref,w_ref,cos_ref,sin_ref,qkv_ref):
    def rt(n,carry):
        o=pl.multiple_of(n*256,256)
        p=dot_nt(n1_ref[...],w_ref[pl.ds(o,256),:])
        for j in range(2):
            x=p[:,128*j:128*j+128]
            qkv_ref[:,pl.ds(pl.multiple_of(o+128*j,128),128)]=(x*cos_ref[...]+swap_halves(x)*sin_ref[...]).astype(bf16)
        return carry
    lax.fori_loop(0,6,rt,0)
    def vt(n,carry):
        o=pl.multiple_of(n*256,256)
        qkv_ref[:,pl.ds(o,256)]=dot_nt(n1_ref[...],w_ref[pl.ds(o,256),:]).astype(bf16)
        return carry
    lax.fori_loop(6,9,vt,0)

def lane_masks(a):
    lane=lax.broadcasted_iota(jnp.int32,a.shape,1)
    z=jnp.zeros_like(a)
    return jnp.where(lane<64,a,z), jnp.where(lane<64,z,a)

def phase_attn_fwd(qkv_ref,p_ref,o_ref):
    L=qkv_ref.shape[0]; QB=256
    def pair(t,carry):
        oq=pl.multiple_of(t*128,128); ok=pl.multiple_of(768+t*128,128); ov=pl.multiple_of(1536+t*128,128)
        for i in range(L//QB):
            kl=(i+1)*QB
            q=lane_masks(qkv_ref[i*QB:(i+1)*QB,pl.ds(oq,128)])
            k=qkv_ref[0:kl,pl.ds(ok,128)]
            v=lane_masks(qkv_ref[0:kl,pl.ds(ov,128)])
            ps=[]
            for h in range(2):
                s=dot_nt(q[h],k)
                row=lax.broadcasted_iota(jnp.int32,s.shape,0)+i*QB
                col=lax.broadcasted_iota(jnp.int32,s.shape,1)
                s=jnp.where(row>=col,s,-1e30)
                m=jnp.max(s,axis=-1,keepdims=True)
                e=jnp.exp2((s-m)*(attn_multiplier*LOG2E))
                pr=(e*(1.0/jnp.sum(e,axis=-1,keepdims=True))).astype(bf16)
                p_ref[2*t+h,i*QB:(i+1)*QB,0:kl]=pr
                ps.append(pr)
            o_ref[i*QB:(i+1)*QB,pl.ds(oq,128)]=dot_nn(jnp.concatenate(ps,1),jnp.concatenate(v,0)).astype(bf16)
        return carry
    lax.fori_loop(0,H//2,pair,0)

def phase_wo_norm2(o_ref,w_ref,x_ref,g_ref,hs_ref,n2_ref):
    L=x_ref.shape[0]; R=128
    def it(i,carry):
        r=pl.ds(pl.multiple_of(i*R,R),R)
        hs=x_ref[r,:].astype(f32)+dot_nn(o_ref[r,:],w_ref[2304:3072,:])
        hs_ref[r,:]=hs
        inv=norm_block(hs,None)
        n2_ref[r,:]=(hs*inv*g_ref[1:2,:]).astype(bf16)
        return carry
    lax.fori_loop(0,L//R,it,0)

def phase_ff(n2_ref,db2_ref,wff_ref,gff_ref,b2_ref,dn2_ref):
    sh=wff_ref.shape[2]; per=256//sh; nt=wff_ref.shape[0]//per
    def tile(t,carry):
        sl=pl.ds(t*per,per)
        wg=wff_ref[sl,0].reshape(256,768); wu=wff_ref[sl,1].reshape(256,768); wd=wff_ref[sl,2].reshape(256,768)
        n2=n2_ref[...]
        g=dot_nt(n2,wg); u=dot_nt(n2,wu)
        da=dot_nt(db2_ref[...],wd)
        sg=1.0/(1.0+jnp.exp2(g*(-LOG2E)))
        silu=g*sg
        a=(silu*u).astype(bf16)
        dg=(da*u*(sg*(1.0+g*(1.0-sg)))).astype(bf16)
        du=(da*silu).astype(bf16)
        b2=dot_nn(a,wd)
        dn=dot_nn(dg,wg)+dot_nn(du,wu)
        @pl.when(t==0)
        def _():
            b2_ref[...]=b2; dn2_ref[...]=dn
        @pl.when(t>0)
        def _():
            b2_ref[...]+=b2; dn2_ref[...]+=dn
        gff_ref[sl,0]=dot_tn(dg,n2).astype(bf16).reshape(per,sh,768)
        gff_ref[sl,1]=dot_tn(du,n2).astype(bf16).reshape(per,sh,768)
        gff_ref[sl,2]=dot_tn(a,db2_ref[...]).astype(bf16).reshape(per,sh,768)
        return carry
    lax.fori_loop(0,nt,tile,0)

def phase_mid(len_ref,c_ref,hs_ref,b2_ref,dn2_ref,g_ref,out_ref,dhs_ref,db1_ref,gg_ref):
    L=hs_ref.shape[0]
    n=len_ref[0]
    gg_ref[...]=jnp.zeros_like(gg_ref)
    def body(r,o):
        row=lax.broadcasted_iota(jnp.int32,(RB,768),0)+o
        hs=hs_ref[r,:]
        out_ref[r,:]=jnp.where(row<n,hs+b2_ref[r,:],0.0).astype(bf16)
        dy=jnp.where(row<n,c_ref[r,:].astype(f32),0.0)
        inv=norm_block(hs,None)
        dn=dn2_ref[r,:]
        q=dn*g_ref[1:2,:]
        gg_ref[1:2,:]+=jnp.sum(hs*inv*dn,axis=0,keepdims=True)
        dh=dy+(inv*q-hs*inv*inv*inv*jnp.mean(hs*q,axis=-1,keepdims=True))
        dhs_ref[r,:]=dh
        db1_ref[r,:]=dh.astype(bf16)
    rows_loop(L,body)

def phase_db2(len_ref,c_ref,db2_ref):
    n=len_ref[0]
    def body(r,o):
        row=lax.broadcasted_iota(jnp.int32,(RB,768),0)+o
        db2_ref[r,:]=jnp.where(row<n,c_ref[r,:].astype(f32),0.0).astype(bf16)
    rows_loop(c_ref.shape[0],body)

def phase_wo_back(db1_ref,o_ref,w_ref,do_ref,gatt_ref):
    def it(n,carry):
        o=pl.multiple_of(n*256,256)
        do_ref[:,pl.ds(o,256)]=dot_nt(db1_ref[...],w_ref[pl.ds(pl.multiple_of(2304+o,256),256),:]).astype(bf16)
        gatt_ref[pl.ds(pl.multiple_of(2304+o,256),256),:]=dot_tn(o_ref[:,pl.ds(o,256)],db1_ref[...]).astype(bf16)
        return carry
    lax.fori_loop(0,3,it,0)

def phase_attn_bwd(qkv_ref,p_ref,do_ref,cos_ref,sin_ref,dp_ref):
    L=qkv_ref.shape[0]; QB=256
    def pair(t,carry):
        oq=pl.multiple_of(t*128,128); ok=pl.multiple_of(768+t*128,128); ov=pl.multiple_of(1536+t*128,128)
        dkt=None; dvt=None
        for i in range(L//QB):
            kl=(i+1)*QB; r=slice(i*QB,(i+1)*QB)
            q=lane_masks(qkv_ref[r,pl.ds(oq,128)])
            k=lane_masks(qkv_ref[0:kl,pl.ds(ok,128)])
            v=qkv_ref[0:kl,pl.ds(ov,128)]
            do=lane_masks(do_ref[r,pl.ds(oq,128)])
            dss=[]; pls=[]
            for h in range(2):
                pb=p_ref[2*t+h,r,0:kl]
                p=pb.astype(f32)
                if i<L//QB:
                    row=lax.broadcasted_iota(jnp.int32,p.shape,0)+i*QB
                dpr=dot_nt(do[h],v)
                pd=p*dpr
                ds=(pd-p*jnp.sum(pd,axis=-1,keepdims=True)).astype(bf16)
                dss.append(ds); pls.append(pb)
            dq=dot_nn(jnp.concatenate(dss,1),jnp.concatenate(k,0))*attn_multiplier
            c=cos_ref[r,:]; s=sin_ref[r,:]
            dp_ref[r,pl.ds(oq,128)]=(dq*c-swap_halves(dq)*s).astype(bf16)
            a=dot_tn(jnp.concatenate(q,0),jnp.concatenate(dss,0))
            b=dot_tn(jnp.concatenate(do,0),jnp.concatenate(pls,0))
            if dkt is None: dkt,dvt=a,b
            else:
                w=dkt.shape[1]
                dkt=jnp.concatenate([dkt+a[:,:w],a[:,w:]],1); dvt=jnp.concatenate([dvt+b[:,:w],b[:,w:]],1)
        dk=dkt.T*attn_multiplier
        dp_ref[:,pl.ds(ok,128)]=(dk*cos_ref[...]-swap_halves(dk)*sin_ref[...]).astype(bf16)
        dp_ref[:,pl.ds(ov,128)]=dvt.T.astype(bf16)
        return carry
    lax.fori_loop(0,H//2,pair,0)

def phase_dn1(dp_ref,w_ref,x_ref,g_ref,dhs_ref,in_ref,gg_ref):
    L=x_ref.shape[0]; R=128
    def it(i,carry):
        r=pl.ds(pl.multiple_of(i*R,R),R)
        dn=dot_nn(dp_ref[r,:],w_ref[0:2304,:])
        xv=x_ref[r,:].astype(f32)
        inv=norm_block(xv,None)
        gg_ref[0:1,:]+=jnp.sum(xv*inv*dn,axis=0,keepdims=True)
        q=dn*g_ref[0:1,:]
        in_ref[r,:]=(dhs_ref[r,:]+(inv*q-xv*inv*inv*inv*jnp.mean(xv*q,axis=-1,keepdims=True))).astype(bf16)
        return carry
    lax.fori_loop(0,L//R,it,0)

def phase_wqkv_grad(dp_ref,n1_ref,gatt_ref):
    def it(n,carry):
        o=pl.multiple_of(n*256,256)
        gatt_ref[pl.ds(o,256),:]=dot_tn(dp_ref[:,pl.ds(o,256)],n1_ref[...]).astype(bf16)
        return carry
    lax.fori_loop(0,9,it,0)

def k2_kernel(len_ref,x_ref,c_ref,watt_ref,wff_ref,g_ref,cos_ref,sin_ref,
              out_ref,in_ref,gatt_ref,gff_ref,gg_ref,
              n1,qkv,pm,o,hs,n2,db2,b2,dn2,dhs,db1,do,dpj):
    phase_norm1(x_ref,g_ref,n1)
    phase_qkv(n1,watt_ref,cos_ref,sin_ref,qkv)
    phase_attn_fwd(qkv,pm,o)
    phase_wo_norm2(o,watt_ref,x_ref,g_ref,hs,n2)
    phase_db2(len_ref,c_ref,db2)
    phase_ff(n2,db2,wff_ref,gff_ref,b2,dn2)
    phase_mid(len_ref,c_ref,hs,b2,dn2,g_ref,out_ref,dhs,db1,gg_ref)
    phase_wo_back(db1,o,watt_ref,do,gatt_ref)
    phase_attn_bwd(qkv,pm,do,cos_ref,sin_ref,dpj)
    phase_dn1(dpj,watt_ref,x_ref,g_ref,dhs,in_ref,gg_ref)
    phase_wqkv_grad(dpj,n1,gatt_ref)

def k2(length,x,c,watt,wff,gains,cos,sin,kern=k2_kernel):
    L,D=x.shape
    V=pl.BlockSpec(memory_space=pltpu.VMEM)
    vm=lambda *s,dt=bf16: pltpu.VMEM(s,dt)
    return pl.pallas_call(kern,
        out_shape=(jax.ShapeDtypeStruct((L,D),bf16),jax.ShapeDtypeStruct((L,D),bf16),jax.ShapeDtypeStruct(watt.shape,bf16),jax.ShapeDtypeStruct(wff.shape,bf16),jax.ShapeDtypeStruct((8,D),f32)),
        in_specs=[pl.BlockSpec(memory_space=pltpu.SMEM)]+[V]*7,out_specs=(V,)*5,
        scratch_shapes=[vm(L,D),vm(L,3*D),vm(H,L,L),vm(L,D),vm(L,D,dt=f32),vm(L,D),vm(L,D),vm(L,D,dt=f32),vm(L,D,dt=f32),vm(L,D,dt=f32),vm(L,D),vm(L,D),vm(L,3*D)],
        compiler_params=pltpu.CompilerParams(vmem_limit_bytes=63*2**20),
        )(length,x,c,watt,wff,gains,cos,sin)
MESH=pl.DeviceIdType.MESH

class Topo:
    def __init__(s, nf, nd):
        assert nd==4 and nf%2==0
        s.Z=nf//2; s.N=nf*nd
        f=lax.axis_index("fsdp"); d=lax.axis_index("dp")
        s.z=f//2; s.y=lax.rem(f,2); s.x=d//2; s.c=lax.rem(d,2)
        s.me=f*4+d
        c=s.c
        s.y1=s.y+c*(1-2*s.y); s.x1=s.x+(1-c)*(1-2*s.x)
        s.y2=s.y+(1-c)*(1-2*s.y); s.x2=s.x+c*(1-2*s.x)
        s.yb=1-s.y; s.xb=1-s.x; s.cb=1-c
    def slot(s,z,y,x,c): return ((z*2+y)*2+x)*2+c
    def dev(s,z,y,x,c): return (z*2+y, x*2+c)
    def flat(s,i): return (i//4, lax.rem(i,4))
    def zk(s,k): return lax.rem(s.z+k,s.Z)
    @property
    def p1(s): return s.dev(s.z,s.y1,s.x1,s.c)
    @property
    def p2(s): return s.dev(s.z,s.y2,s.x2,s.c)
    @property
    def sib(s): return s.dev(s.z,s.y,s.x,s.cb)

def loop(lo,hi,body):
    lax.fori_loop(lo,hi,lambda i,c:(body(i),c)[1],0)

def rcopy(src,dst,ssem,rsem,dev):
    return pltpu.make_async_remote_copy(src_ref=src,dst_ref=dst,send_sem=ssem,recv_sem=rsem,device_id=dev,device_id_type=MESH)

def wait_bytes(ref,sem):
    pltpu.make_async_copy(ref,ref,sem).wait()

def barrier_all(t):
    b=pltpu.get_barrier_semaphore()
    def sig(k): pl.semaphore_signal(b,inc=1,device_id=t.flat(lax.rem(t.me+k,t.N)),device_id_type=MESH)
    loop(1,t.N,sig)
    pl.semaphore_wait(b,t.N-1)

class A2A:
    def __init__(s,t,src,dst,ssem,rsem,lsem): s.t,s.src,s.dst,s.ssem,s.rsem,s.lsem=t,src,dst,ssem,rsem,lsem
    def start(s):
        t=s.t
        pltpu.make_async_copy(s.src.at[t.me],s.dst.at[t.me],s.lsem).start()
        def f(k):
            d=lax.rem(t.me+k,t.N)
            rcopy(s.src.at[d],s.dst.at[t.me],s.ssem,s.rsem,t.flat(d)).start()
        loop(1,t.N,f)
    def wait_recv(s):
        n=s.t.N-1
        pltpu.make_async_copy(s.src.at[s.t.me],s.dst.at[s.t.me],s.lsem).wait()
        wait_bytes(s.dst.at[pl.ds(0,n)],s.rsem)
    def wait_send(s):
        wait_bytes(s.src.at[pl.ds(0,s.t.N-1)],s.ssem)

class Gather:
    def __init__(s,t,src,dst,ssem,rsem,lsem): s.t,s.src,s.dst,s.ssem,s.rsem,s.lsem=t,src,dst,ssem,rsem,lsem
    def send(s,slot,dev,src=None):
        rcopy(s.dst.at[slot] if src is None else src,s.dst.at[slot],s.ssem,s.rsem.at[slot],dev).start()
    def wait(s,slot):
        wait_bytes(s.dst.at[slot],s.rsem.at[slot])
    def start(s):
        t=s.t
        pltpu.make_async_copy(s.src,s.dst.at[t.me],s.lsem).start()
        for dev in (t.p1,t.p2,t.sib): s.send(t.me,dev,s.src)
        loop(1,t.Z,lambda k: s.send(t.me,t.dev(t.zk(k),t.y,t.x,t.c),s.src))
    def phase1(s):
        t=s.t
        def f(k):
            sl=t.slot(t.zk(k),t.y,t.x,t.c); s.wait(sl)
            for dev in (t.p1,t.p2,t.sib): s.send(sl,dev)
        loop(1,t.Z,f)
    def phase2(s):
        t=s.t
        def f(k):
            sl=t.slot(t.zk(k),t.y1,t.x1,t.c); s.wait(sl)
            for dev in (t.p2,t.sib): s.send(sl,dev)
        loop(0,t.Z,f)
    def phase3(s):
        t=s.t
        for y,x in ((t.y2,t.x2),(t.yb,t.xb)):
            def f(k):
                sl=t.slot(t.zk(k),y,x,t.c); s.wait(sl); s.send(sl,t.sib)
            loop(0,t.Z,f)
    def phase4(s):
        t=s.t
        for y,x in ((0,0),(0,1),(1,0),(1,1)):
            loop(0,t.Z,lambda k: s.wait(t.slot(t.zk(k),y,x,t.cb)))
    def finish(s):
        t=s.t
        pltpu.make_async_copy(s.src,s.dst.at[t.me],s.lsem).wait()
        wait_bytes(s.dst.at[pl.ds(0,t.N-1)],s.ssem)

def k1_kernel(nf,nd,perm,tok,cot0,gn,att,ff,xg,cg,gg,wa,wf,cot,ss,rs,ls,ars,frs):
    t=Topo(nf,nd)
    barrier_all(t)
    tk=A2A(t,tok,xg,ss.at[0],rs.at[0],ls.at[0])
    ct=A2A(t,cot,cg,ss.at[1],rs.at[1],ls.at[1])
    A=Gather(t,att,wa,ss.at[3],ars,ls.at[3]); F=Gather(t,ff,wf,ss.at[4],frs,ls.at[4])
    pltpu.make_async_copy(gn,gg.at[t.me],ls.at[2]).start()
    def gs(k): rcopy(gn,gg.at[t.me],ss.at[2],rs.at[2],t.flat(lax.rem(t.me+k,t.N))).start()
    loop(1,t.N,gs)
    A.start()
    tk.start()
    def pm(i): cot[i]=cot0[perm[i]]
    loop(0,t.N,pm)
    A.phase1()
    F.start()
    A.phase2()
    F.phase1()
    A.phase3()
    F.phase2()
    ct.start()
    A.phase4()
    F.phase3(); F.phase4()
    tk.wait_recv(); ct.wait_recv()
    pltpu.make_async_copy(gn,gg.at[t.me],ls.at[2]).wait()
    wait_bytes(gg.at[pl.ds(0,t.N-1)],rs.at[2]); wait_bytes(gg.at[pl.ds(0,t.N-1)],ss.at[2])
    A.finish(); F.finish(); tk.wait_send(); ct.wait_send()

def k1(perm,tok,cot,gn,att,ff):
    nf,nd=lax.axis_size("fsdp"),lax.axis_size("dp"); N=nf*nd
    anyv=pl.BlockSpec(memory_space=pl.ANY); D=pltpu.SemaphoreType.DMA
    sd=jax.ShapeDtypeStruct
    return pl.pallas_call(functools.partial(k1_kernel,nf,nd),
        out_shape=(sd(tok.shape,tok.dtype),sd(cot.shape,cot.dtype),sd((N,)+gn.shape,gn.dtype),sd((N,)+att.shape,att.dtype),sd((N,)+ff.shape,ff.dtype)),
        in_specs=[pl.BlockSpec(memory_space=pltpu.SMEM),anyv,pl.BlockSpec(memory_space=pltpu.VMEM),anyv,anyv,anyv],out_specs=(anyv,)*5,
        scratch_shapes=[pltpu.VMEM(cot.shape,cot.dtype),D((5,)),D((5,)),D((5,)),D((N,)),D((N,))],
        compiler_params=pltpu.CompilerParams(collective_id=0,has_side_effects=True))(perm,tok,cot,gn,att,ff)

class Scatter:
    def __init__(s,t,g,rc,r1,r2,rz,ss,rcs,r1s,r2s,rzs):
        s.t,s.g,s.rc,s.r1,s.r2,s.rz,s.ss,s.rcs,s.r1s,s.r2s,s.rzs=t,g,rc,r1,r2,rz,ss,rcs,r1s,r2s,rzs
        s.Z=t.Z
    def groups(s,sibling):
        t=s.t
        if sibling:
            return ((t.yb,t.xb),(t.y1,t.x1),(t.y2,t.x2),(t.y,t.x))
        return ((t.yb,t.xb),(t.y2,t.x2),(t.y1,t.x1),(t.y,t.x))
    def start(s):
        t=s.t; Z=s.Z
        for gi,(y,x) in enumerate(s.groups(True)):
            def f(k):
                rcopy(s.g.at[t.slot(t.zk(k),y,x,t.cb)],s.rc.at[gi*Z+k],s.ss.at[0],s.rcs.at[gi*Z+k],t.sib).start()
            loop(0,Z,f)
    def stage_c(s):
        t=s.t; Z=s.Z
        for gi,(y,x) in enumerate(s.groups(False)):
            def f(k):
                j=gi*Z+k
                wait_bytes(s.rc.at[j],s.rcs.at[j])
                s.rc[j]=s.rc[j]+s.g[t.slot(t.zk(k),y,x,t.c)]
                if gi<2: rcopy(s.rc.at[j],s.r1.at[j],s.ss.at[1],s.r1s.at[j],t.p2).start()
            loop(0,Z,f)
    def stage_1(s):
        t=s.t; Z=s.Z
        for gi in range(2):
            def f(k):
                j=gi*Z+k
                wait_bytes(s.r1.at[j],s.r1s.at[j])
                s.r1[j]=s.r1[j]+s.rc[2*Z+j]
                if gi==0: rcopy(s.r1.at[j],s.r2.at[k],s.ss.at[2],s.r2s.at[k],t.p1).start()
            loop(0,Z,f)
    def stage_2(s):
        t=s.t; Z=s.Z
        def f(k):
            wait_bytes(s.r2.at[k],s.r2s.at[k])
            s.r2[k]=s.r2[k]+s.r1[Z+k]
            rcopy(s.r2.at[k],s.rz.at[Z-k-1],s.ss.at[3],s.rzs.at[Z-k-1],t.dev(t.zk(k),t.y,t.x,t.c)).start()
        loop(1,Z,f)
        wait_bytes(s.r2.at[0],s.r2s.at[0])
    def final(s,out):
        Z=s.Z
        tot=s.r2[0].astype(f32)+s.r1[Z].astype(f32)
        for k in range(Z-1):
            wait_bytes(s.rz.at[k],s.rzs.at[k])
            tot=tot+s.rz[k].astype(f32)
        out[...]=tot
    def wait_send(s):
        Z=s.Z
        wait_bytes(s.rc,s.ss.at[0])
        wait_bytes(s.r1,s.ss.at[1])
        wait_bytes(s.r2,s.ss.at[2])
        wait_bytes(s.rz,s.ss.at[3])

def k3_kernel(nf,nd,perm,orow,irow,gg,ga,gf,oo0,io,ggo,ao,fo,oo,ggr,arc,ar1,ar2,arz,frc,fr1,fr2,frz,ss,rs,ls,ass,fss,acs,a1s,a2s,azs,fcs,f1s,f2s,fzs):
    t=Topo(nf,nd)
    barrier_all(t)
    A=Scatter(t,ga,arc,ar1,ar2,arz,ass,acs,a1s,a2s,azs)
    F=Scatter(t,gf,frc,fr1,fr2,frz,fss,fcs,f1s,f2s,fzs)
    F.start(); A.start()
    pltpu.make_async_copy(gg.at[t.me],ggr.at[t.me],ls.at[2]).start()
    def gs(k):
        d=lax.rem(t.me+k,t.N)
        rcopy(gg.at[d],ggr.at[t.me],ss.at[2],rs.at[2],t.flat(d)).start()
    loop(1,t.N,gs)
    F.stage_c()
    o=A2A(t,orow,oo,ss.at[0],rs.at[0],ls.at[0])
    i=A2A(t,irow,io,ss.at[1],rs.at[1],ls.at[1])
    o.start()
    A.stage_c()
    i.start()
    F.stage_1(); F.stage_2()
    A.stage_1(); A.stage_2()
    pltpu.make_async_copy(gg.at[t.me],ggr.at[t.me],ls.at[2]).wait()
    wait_bytes(ggr.at[pl.ds(0,t.N-1)],rs.at[2]); wait_bytes(ggr.at[pl.ds(0,t.N-1)],ss.at[2])
    tot=ggr[0]
    for k in range(1,t.N): tot=tot+ggr[k]
    ggo[...]=tot
    F.final(fo); A.final(ao)
    o.wait_recv()
    def pm(j): oo0[j]=oo[perm[j]]
    loop(0,t.N,pm)
    i.wait_recv(); o.wait_send(); i.wait_send()
    F.wait_send(); A.wait_send()

def k3(perm,orow,irow,gg,ga,gf):
    nf,nd=lax.axis_size("fsdp"),lax.axis_size("dp"); N=nf*nd; Z=nf//2
    anyv=pl.BlockSpec(memory_space=pl.ANY); V=pl.BlockSpec(memory_space=pltpu.VMEM); D=pltpu.SemaphoreType.DMA
    sd=jax.ShapeDtypeStruct
    ash,fsh=ga.shape[1:],gf.shape[1:]
    vm=lambda n,sh: pltpu.VMEM((n,)+sh,bf16)
    return pl.pallas_call(functools.partial(k3_kernel,nf,nd),
        out_shape=(sd(orow.shape,bf16),sd(irow.shape,bf16),sd(gg.shape[1:],f32),sd(ash,f32),sd(fsh,f32)),
        in_specs=[pl.BlockSpec(memory_space=pltpu.SMEM),anyv,anyv,V,V,V],out_specs=(V,anyv,V,V,V),
        scratch_shapes=[pltpu.VMEM(orow.shape,bf16),pltpu.VMEM(gg.shape,f32)]+[vm(n,sh) for sh in (ash,fsh) for n in (4*Z,2*Z,Z,Z-1)]+[D((3,)),D((3,)),D((3,)),D((4,)),D((4,))]+[D((n,)) for _ in range(2) for n in (4*Z,2*Z,Z,Z-1)],
        compiler_params=pltpu.CompilerParams(collective_id=1,has_side_effects=True,vmem_limit_bytes=60*2**20))(perm,orow,irow,gg,ga,gf)


from jax.sharding import PartitionSpec as P
AX = ("fsdp", "dp")
beta_first = 0.5
beta_second = 0.5
learning_rate = 0.03
weight_decay = 0.1
adam_epsilon = 1e-08


def adam_update(master, gradient, first_moment, second_moment, decay):
    first_new = beta_first * first_moment + (1.0 - beta_first) * gradient
    second_new = beta_second * second_moment + (1.0 - beta_second) * gradient * gradient
    first_hat = first_new / (1.0 - beta_first**STEP)
    second_hat = second_new / (1.0 - beta_second**STEP)
    master_new = master - learning_rate * (
        first_hat / (jnp.sqrt(second_hat) + adam_epsilon) + decay * master
    )
    return (first_new, second_new, master_new)


def local(tokens, cotangent, lengths, device_sequence, slot_device, attention_master, feedforward_master, gains_master,
          attention_mean, attention_square, feedforward_mean, feedforward_square, gains_mean, gains_square):
    N = lax.axis_size(AX)
    me = lax.axis_index(AX)
    positions, width = tokens.shape[1], tokens.shape[2]
    length = positions * N
    gl = gains_master.shape[1]
    counter = jnp.arange(N, dtype=jnp.int32)
    slot_sequence = jnp.sum(jnp.where(slot_device[:, None] == counter[None, :], device_sequence[None, :], 0), axis=1)
    slot_of_sequence = jnp.sum(jnp.where(slot_sequence[:, None] == counter[None, :], counter[:, None], 0), axis=0)
    att_low = attention_master.astype(bf16)
    ff_low = feedforward_master.transpose(1, 0, 2).astype(bf16)
    gn = jnp.zeros((8, 128), f32).at[:2, :gl].set(gains_master.astype(bf16).astype(f32))
    xg, cg, gg, wa, wf = k1(slot_of_sequence, tokens, cotangent, gn, att_low, ff_low)
    gains = jnp.zeros((8, width), f32).at[:2].set(gg[:, :2, :gl].transpose(1, 0, 2).reshape(2, width))
    C, S = tables(length)
    orow, irow, gatt, gff, ggr = k2(jnp.sum(jnp.where(counter == me, lengths, 0))[None], xg.reshape(length, width), cg.reshape(length, width),
                                    wa.reshape(-1, width), wf, gains, jnp.asarray(C), jnp.asarray(S))
    gblocks = jnp.zeros((N, 8, 128), f32).at[:, :2, :gl].set(ggr[:2].reshape(2, N, gl).transpose(1, 0, 2))
    oo, io, gsum, ag, fg = k3(slot_sequence, orow.reshape(N, positions, width), irow.reshape(N, positions, width), gblocks,
                              gatt.reshape(N, -1, width), gff)
    output = oo
    attention_gradient = ag
    feedforward_gradient = fg.transpose(1, 0, 2)
    gains_gradient = gsum[:2, :gl]
    mean_attention, square_attention, master_attention = adam_update(
        attention_master, attention_gradient, attention_mean, attention_square, weight_decay)
    mean_feedforward, square_feedforward, master_feedforward = adam_update(
        feedforward_master, feedforward_gradient, feedforward_mean, feedforward_square, weight_decay)
    mean_gains, square_gains, master_gains = adam_update(gains_master, gains_gradient, gains_mean, gains_square, 0.0)
    return (output, io, attention_gradient, feedforward_gradient, gains_gradient, mean_attention, square_attention,
            mean_feedforward, square_feedforward, mean_gains, square_gains, master_attention, master_feedforward,
            master_gains - gains_master, master_attention.astype(bf16), master_feedforward.astype(bf16))


def solution(mesh):
    t, r, f, g = P(None, AX, None), P(AX, None), P(AX, None, None), P(None, AX)
    in_specs = (t, t, P(), P(), P(), r, f, g, r, r, f, f, g, g)
    out_specs = (t, t, r, f, g, r, r, f, f, g, g, r, f, g, r, f)
    return jax.shard_map(local, mesh=mesh, in_specs=in_specs, out_specs=out_specs, check_vma=False)
```

time: 620 us -> 306 us (0.49); the launches traced: 609 us -> 305 us
  waiting for transfers between devices: 296 us -> 0 us
  Pallas kernels: 0 us -> 282 us
  blocking collectives: 100 us -> 0 us
  matrix products: 75.5 us -> 0 us
  other arithmetic: 63.5 us -> 13.5 us
  local copies, waits for them, and re-layouts: 34.3 us -> 9.02 us
  starting transfers between devices: 21.6 us -> 0 us
  between operations: 17.3 us -> 0.83 us
    pallas_call x0 -> x3, Pallas kernels: none -> 282 us  [the longest x1 110 us: k1(): pl.pallas_call(functools.partial(k1_kernel, nf, nd), out_shape=(sd(tok.sh...]
    reduce_scatter x2 -> x0, waiting for transfers between devices: 235 us -> none  [the longest x1 209 us: local(): lax.psum_scatter(jnp.stack([times_tokens(gate_grad, normed_two), times_to...]
    dot_general x21 -> x0, matrix products: 75.5 us -> none  [the longest x5 19.7 us: times_rows(): lax.dot_general(left, right, (((1,), (1,)), ((), ())), preferred_element_...]
    all_gather x1 -> x0, blocking collectives: 51.3 us -> none  [local(): lax.all_gather(gains_low, ('fsdp', 'dp'), axis=1, tiled=True)]
    unnamed x1 -> x0, blocking collectives: 48.8 us -> none
    all_to_all x4 -> x0, waiting for transfers between devices: 32.4 us -> none  [the longest x1 21.6 us: local(): lax.all_to_all(sent_tokens, ('fsdp', 'dp'), split_axis=0, concat_axis=1,...]
    all_gather x2 -> x0, waiting for transfers between devices: 28.6 us -> none  [the longest x1 28.6 us: local(): lax.all_gather(feedforward_low, ('fsdp', 'dp'), axis=0, tiled=True)]
    all_to_all x4 -> x0, starting transfers between devices: 21.5 us -> none  [the longest x1 7.47 us: local(): lax.all_to_all(input_rows.reshape(1, length, width), ('fsdp', 'dp'), spli...]
  transfers between devices with their start and end apart: 8 -> 0, of which waited for: 5 -> 0; matrix products, arithmetic and copies ran while one was open for 15% -> 0% of each run, Pallas kernels for 0% -> 0%
where the time goes in v1:
time: 306 us; the launch traced here: 305 us
  Pallas kernels  282 us (92%)
  other arithmetic  13.5 us (4%)
  local copies, waits for them, and re-layouts  9.02 us (3%)
    pallas_call x1, Pallas kernels, k1(): pl.pallas_call(functools.partial(k1_kernel, nf, nd), out_shape=(sd(tok.sh...  110 us
    pallas_call x1, Pallas kernels, k3(): pl.pallas_call(functools.partial(k3_kernel, nf, nd), out_shape=(sd(orow.s...  106 us
    pallas_call x1, Pallas kernels, k2(): pl.pallas_call(kern, out_shape=(jax.ShapeDtypeStruct((L, D), bf16), jax.S...  66.1 us

profile of v1, /device:TPU:8, one launch (start us, length us, event | category | flops | bytes accessed | tf_op | source)
XLA Modules:
  0.0 305.4 jit_solution(1566555433217225571)
XLA Ops:
  0.7 1.3 fusion.3
  1.9 0.8 select_reduce_fusion.1.perm
  2.8 0.0 copy-start.11
  2.8 0.6 select_reduce_fusion.perm
  3.4 0.7 convert_element_type.18
  4.1 0.6 pad_convert_fusion.gn
  4.7 1.6 convert_element_type.19.att
  6.3 1.8 convert_bitcast_fusion.ff
  8.1 109.5 %shard_map.279 = (bf16[32,16,768]{2,1,0:T(8,128)(2,1)}, bf16[32,16,768]{2,1,0:T(8,128)(2,1)}, f32[32,8,128]{2,1,0:T(8,128)}, bf16[32,96,768]{2,1,0:T(8,128)(2,1)}, bf16[32,3,64,768]{3,2,1,0:T(8,128)(2,1)}) custom-call(s32[32]{0:T(128)} %select_reduce_fusion.perm, bf16[32,16,768]{2,1,0:T(8,128)(2,1)} %tok.1, bf16[32,16,768]{2,1,0:T(8,128)(2,1)} %cot0.1, ...), custom_call_target="tpu_custom_call" | custom-call | tf_op jit(solution)/shard_map/pallas_call | solution.py:369
  117.7 0.9 slice_bitcast_fusion
  118.6 0.1 reshape.152
  118.7 0.6 scatter.19.g_ref
  119.3 66.1 %shard_map.280 = (bf16[512,768]{1,0:T(8,128)(2,1)}, bf16[512,768]{1,0:T(8,128)(2,1)}, bf16[3072,768]{1,0:T(8,128)(2,1)}, bf16[32,3,64,768]{3,2,1,0:T(8,128)(2,1)}, f32[8,768]{1,0:T(8,128)}) custom-call(s32[1]{0:T(128)} %bitcast.len_ref, bf16[512,768]{1,0:T(8,128)(2,1)} %bitcast.21, bf16[512,768]{1,0:T(8,128)(2,1)} %bitcast.22, bf16[3072,768]{1,0:T(8,128)(2,1)} %bitcast.17, ...), custom_call_target="tpu_custom_call" | custom-call | tf_op jit(solution)/shard_map/pallas_call | solution.py:239
  185.4 0.0 copy-done.11
  185.4 0.0 copy-start.8
  185.4 0.0 copy-start.9
  185.4 0.0 copy-start.10
  185.4 0.0 copy-start.2
  185.4 0.0 copy-start.6
  185.4 0.0 copy-start.7
  185.4 0.0 copy-start
  185.5 0.0 copy-start.4
  185.5 0.0 copy-start.5
  185.5 0.9 slice.71
  186.4 0.1 reshape.155
  186.5 0.7 scatter.20.gg
  187.2 106.4 %shard_map.281 = (bf16[32,16,768]{2,1,0:T(8,128)(2,1)}, bf16[32,16,768]{2,1,0:T(8,128)(2,1)}, f32[8,128]{1,0:T(8,128)}, f32[96,768]{1,0:T(8,128)}, f32[3,64,768]{2,1,0:T(8,128)}) custom-call(s32[32]{0:T(128)} %copy-done.11, bf16[32,16,768]{2,1,0:T(8,128)(2,1)} %bitcast.19, bf16[32,16,768]{2,1,0:T(8,128)(2,1)} %bitcast.20, f32[32,8,128]{2,1,0:T(8,128)} %scatter.20.gg, ...), custom_call_target="tpu_custom_call" | custom-call | tf_op jit(solution)/shard_map/pallas_call | solution.py:467
  293.6 0.0 copy-start.3
  293.6 0.0 copy-start.1
  293.6 0.0 copy-done.8
  293.6 0.0 copy-done.9
  293.6 0.0 copy-done.10
  293.6 1.3 subtract_subtract_fusion
  294.9 0.0 copy-done.2
  295.0 0.0 copy-done.6
  295.0 0.0 copy-done.7
  295.0 2.1 fusion.6
  297.0 0.0 copy-done
  297.0 0.0 copy-done.4
  297.0 0.0 copy-done.5
  297.0 2.7 fusion.4
  299.7 2.1 copy.43
  301.8 2.1 copy.44
  303.8 0.0 copy-done.3
  303.8 0.7 copy.45
  304.6 0.0 copy-done.1
  304.6 0.8 copy.46
  (2 shorter events, 0.0 us)
Async XLA Ops:
  2.8 182.6 %copy-start.11 = (s32[32]{0:T(128)}, s32[32]{0:T(128)S(1)}, u32[]{:S(2)}) copy-start(s32[32]{0:T(128)S(1)} %select_reduce_fusion.1.perm) | copy-start | bytes 388
  185.4 108.2 %copy-start.8 = (f32[2,24]{1,0:T(2,128)S(1)}, f32[2,24]{1,0:T(2,128)}, u32[]{:S(2)}) copy-start(f32[2,24]{1,0:T(2,128)} %param.29) | copy-start | bytes 580
  185.4 108.2 %copy-start.9 = (f32[2,24]{1,0:T(2,128)S(1)}, f32[2,24]{1,0:T(2,128)}, u32[]{:S(2)}) copy-start(f32[2,24]{1,0:T(2,128)} %param.35) | copy-start | bytes 580
  185.4 108.2 %copy-start.10 = (f32[2,24]{1,0:T(2,128)S(1)}, f32[2,24]{1,0:T(2,128)}, u32[]{:S(2)}) copy-start(f32[2,24]{1,0:T(2,128)} %param.34) | copy-start | bytes 580
  185.4 109.5 %copy-start.2 = (f32[96,768]{1,0:T(8,128)S(1)}, f32[96,768]{1,0:T(8,128)}, u32[]{:S(2)}) copy-start(f32[96,768]{1,0:T(8,128)} %param.27) | copy-start | bytes 884740
  185.4 109.5 %copy-start.6 = (f32[96,768]{1,0:T(8,128)S(1)}, f32[96,768]{1,0:T(8,128)}, u32[]{:S(2)}) copy-start(f32[96,768]{1,0:T(8,128)} %param.31) | copy-start | bytes 884740
  185.4 109.5 %copy-start.7 = (f32[96,768]{1,0:T(8,128)S(1)}, f32[96,768]{1,0:T(8,128)}, u32[]{:S(2)}) copy-start(f32[96,768]{1,0:T(8,128)} %param.30) | copy-start | bytes 884740
  185.4 111.6 %copy-start = (f32[64,3,768]{2,0,1:T(8,128)S(1)}, f32[64,3,768]{2,0,1:T(8,128)}, u32[]{:S(2)}) copy-start(f32[64,3,768]{2,0,1:T(8,128)} %param.28) | copy-start | bytes 1769476
  185.5 111.6 %copy-start.4 = (f32[64,3,768]{2,0,1:T(8,128)S(1)}, f32[64,3,768]{2,0,1:T(8,128)}, u32[]{:S(2)}) copy-start(f32[64,3,768]{2,0,1:T(8,128)} %param.33) | copy-start | bytes 1769476
  185.5 111.6 %copy-start.5 = (f32[64,3,768]{2,0,1:T(8,128)S(1)}, f32[64,3,768]{2,0,1:T(8,128)}, u32[]{:S(2)}) copy-start(f32[64,3,768]{2,0,1:T(8,128)} %param.32) | copy-start | bytes 1769476
  293.6 10.3 %copy-start.3 = (f32[96,768]{1,0:T(8,128)S(1)}, f32[96,768]{1,0:T(8,128)}, u32[]{:S(2)}) copy-start(f32[96,768]{1,0:T(8,128)} %get-tuple-element.112) | copy-start | bytes 884740
  293.6 11.0 %copy-start.1 = (f32[3,64,768]{2,1,0:T(8,128)S(1)}, f32[3,64,768]{2,1,0:T(8,128)}, u32[]{:S(2)}) copy-start(f32[3,64,768]{2,1,0:T(8,128)} %get-tuple-element.80) | copy-start | bytes 1769476

commit v2 on v1

--- a/solution.py
+++ b/solution.py
@@ -526,8 +526,380 @@
             master_gains - gains_master, master_attention.astype(bf16), master_feedforward.astype(bf16))
 
 
+class Topo2(Topo):
+    def __init__(s, nf, nd):
+        super().__init__(nf, nd)
+    def flip(s, gi, cc):
+        a, b = lax.rem(gi, 2), gi // 2
+        fx, fy = (1 - cc) * a + cc * b, (1 - cc) * b + cc * a
+        return s.y + fy * (1 - 2 * s.y), s.x + fx * (1 - 2 * s.x)
+    def g8(s, gi, cc):
+        y, x = s.flip(gi, cc)
+        return (y * 2 + x) * 2 + cc
+
+
+class Gather2:
+    def __init__(s, t, at, ssem, rsem): s.t, s.at, s.ssem, s.rsem = t, at, ssem, rsem
+    def send(s, z, g, dev):
+        rcopy(s.at(z, g), s.at(z, g), s.ssem, s.rsem.at[z, g], dev).start()
+    def wait(s, z, g): wait_bytes(s.at(z, g), s.rsem.at[z, g])
+    def start(s):
+        t = s.t; g = t.g8(0, t.c)
+        loop(1, t.Z, lambda k: s.send(t.z, g, t.dev(t.zk(k), t.y, t.x, t.c)))
+        for dev in (t.p1, t.p2, t.sib): s.send(t.z, g, dev)
+    def take(s, gi, lo=0, hi=None):
+        t = s.t; g = t.g8(gi, t.c)
+        to = {0: (t.p1, t.p2, t.sib), 1: (t.p2, t.sib)}.get(gi, (t.sib,))
+        def f(k):
+            z = t.zk(k); s.wait(z, g)
+            for dev in to: s.send(z, g, dev)
+        loop(lo, t.Z if hi is None else hi, f)
+    def take_sib(s, gi):
+        t = s.t; g = t.g8(gi, t.cb)
+        loop(0, t.Z, lambda k: s.wait(t.zk(k), g))
+
+
+class Scatter2:
+    def __init__(s, t, at, ld, rc, r1, r2, rz, ss, rcs, r1s, r2s, rzs):
+        s.t, s.at, s.ld, s.rc, s.r1, s.r2, s.rz, s.ss, s.rcs, s.r1s, s.r2s, s.rzs = t, at, ld, rc, r1, r2, rz, ss, rcs, r1s, r2s, rzs
+        s.Z = t.Z
+    def start(s, gi):
+        t = s.t; Z = s.Z; g = t.g8(gi, t.cb)
+        def f(k):
+            j = (3 - gi) * Z + k
+            rcopy(s.at(t.zk(k), g), s.rc.at[j], s.ss.at[0], s.rcs.at[j], t.sib).start()
+        loop(0, Z, f)
+    def stage_c(s, gi):
+        t = s.t; Z = s.Z; g = t.g8(gi, t.c)
+        def f(k):
+            j = (3 - gi) * Z + k
+            wait_bytes(s.rc.at[j], s.rcs.at[j])
+            s.rc[j] = s.rc[j] + s.ld(t.zk(k), g)
+            if gi >= 2: rcopy(s.rc.at[j], s.r1.at[j], s.ss.at[1], s.r1s.at[j], t.p2).start()
+        loop(0, Z, f)
+    def stage_1(s, h):
+        t = s.t; Z = s.Z
+        def f(k):
+            j = h * Z + k
+            wait_bytes(s.r1.at[j], s.r1s.at[j])
+            s.r1[j] = s.r1[j] + s.rc[2 * Z + j]
+            if h == 0: rcopy(s.r1.at[j], s.r2.at[k], s.ss.at[2], s.r2s.at[k], t.p1).start()
+        loop(0, Z, f)
+    def stage_2(s):
+        t = s.t; Z = s.Z
+        def f(k):
+            wait_bytes(s.r2.at[k], s.r2s.at[k])
+            s.r2[k] = s.r2[k] + s.r1[Z + k]
+            rcopy(s.r2.at[k], s.rz.at[Z - k - 1], s.ss.at[3], s.rzs.at[Z - k - 1], t.dev(t.zk(k), t.y, t.x, t.c)).start()
+        loop(1, Z, f)
+        wait_bytes(s.r2.at[0], s.r2s.at[0])
+    def final(s, out):
+        Z = s.Z
+        tot = s.r2[0].astype(f32) + s.r1[Z].astype(f32)
+        for k in range(Z - 1):
+            wait_bytes(s.rz.at[k], s.rzs.at[k])
+            tot = tot + s.rz[k].astype(f32)
+        out[...] = tot
+    def wait_send(s):
+        wait_bytes(s.rc, s.ss.at[0]); wait_bytes(s.r1, s.ss.at[1]); wait_bytes(s.r2, s.ss.at[2]); wait_bytes(s.rz, s.ss.at[3])
+
+
+class Exchange:
+    def __init__(s, t, src, dst, sbulk, dbulk, ssem, rsem, lsem):
+        s.t, s.src, s.dst, s.sbulk, s.dbulk, s.ssem, s.rsem, s.lsem = t, src, dst, sbulk, dbulk, ssem, rsem, lsem
+    def start(s):
+        t = s.t
+        pltpu.make_async_copy(s.src(t.me), s.dst(t.me), s.lsem).start()
+        def f(k):
+            d = lax.rem(t.me + k, t.N)
+            rcopy(s.src(d), s.dst(t.me), s.ssem, s.rsem, t.flat(d)).start()
+        loop(1, t.N, f)
+    def wait_recv(s):
+        pltpu.make_async_copy(s.src(s.t.me), s.dst(s.t.me), s.lsem).wait()
+        wait_bytes(s.dbulk, s.rsem)
+    def wait_send(s): wait_bytes(s.sbulk, s.ssem)
+
+
+def rows_of(ref, n):
+    return lambda d: ref.at[pl.ds(pl.multiple_of(d * n, n), n)]
+
+
+def attn_fwd2(qkv_ref, ps, o_ref, lo, hi):
+    QB = 256
+    def pair(t, carry):
+        oq = pl.multiple_of(t * 128, 128); ok = pl.multiple_of(768 + t * 128, 128); ov = pl.multiple_of(1536 + t * 128, 128)
+        for i in range(len(ps)):
+            kl = (i + 1) * QB
+            q = lane_masks(qkv_ref[i * QB:kl, pl.ds(oq, 128)])
+            k = qkv_ref[0:kl, pl.ds(ok, 128)]
+            v = lane_masks(qkv_ref[0:kl, pl.ds(ov, 128)])
+            got = []
+            for h in range(2):
+                s = dot_nt(q[h], k)
+                row = lax.broadcasted_iota(jnp.int32, s.shape, 0) + i * QB
+                col = lax.broadcasted_iota(jnp.int32, s.shape, 1)
+                s = jnp.where(row >= col, s, -1e30)
+                m = jnp.max(s, axis=-1, keepdims=True)
+                e = jnp.exp2((s - m) * (attn_multiplier * LOG2E))
+                pr = (e * (1.0 / jnp.sum(e, axis=-1, keepdims=True))).astype(bf16)
+                ps[i][2 * t + h] = pr
+                got.append(pr)
+            o_ref[i * QB:kl, pl.ds(oq, 128)] = dot_nn(jnp.concatenate(got, 1), jnp.concatenate(v, 0)).astype(bf16)
+        return carry
+    lax.fori_loop(lo, hi, pair, 0)
+
+
+def attn_bwd2(qkv_ref, ps, do_ref, cos_ref, sin_ref, lo, hi):
+    QB = 256
+    def pair(t, carry):
+        oq = pl.multiple_of(t * 128, 128); ok = pl.multiple_of(768 + t * 128, 128); ov = pl.multiple_of(1536 + t * 128, 128)
+        dkt = None; dvt = None
+        for i in range(len(ps)):
+            kl = (i + 1) * QB; r = slice(i * QB, kl)
+            q = lane_masks(qkv_ref[r, pl.ds(oq, 128)])
+            k = lane_masks(qkv_ref[0:kl, pl.ds(ok, 128)])
+            v = qkv_ref[0:kl, pl.ds(ov, 128)]
+            do = lane_masks(do_ref[r, pl.ds(oq, 128)])
+            dss = []; pls = []
+            for h in range(2):
+                pb = ps[i][2 * t + h]
+                p = pb.astype(f32)
+                pd = p * dot_nt(do[h], v)
+                dss.append((pd - p * jnp.sum(pd, axis=-1, keepdims=True)).astype(bf16)); pls.append(pb)
+            dq = dot_nn(jnp.concatenate(dss, 1), jnp.concatenate(k, 0)) * attn_multiplier
+            a = dot_tn(jnp.concatenate(q, 0), jnp.concatenate(dss, 0))
+            b = dot_tn(jnp.concatenate(do, 0), jnp.concatenate(pls, 0))
+            qkv_ref[r, pl.ds(oq, 128)] = (dq * cos_ref[r, :] - swap_halves(dq) * sin_ref[r, :]).astype(bf16)
+            if dkt is None: dkt, dvt = a, b
+            else:
+                w = dkt.shape[1]
+                dkt = jnp.concatenate([dkt + a[:, :w], a[:, w:]], 1); dvt = jnp.concatenate([dvt + b[:, :w], b[:, w:]], 1)
+        dk = dkt.T * attn_multiplier
+        qkv_ref[:, pl.ds(ok, 128)] = (dk * cos_ref[...] - swap_halves(dk) * sin_ref[...]).astype(bf16)
+        qkv_ref[:, pl.ds(ov, 128)] = dvt.T.astype(bf16)
+        return carry
+    lax.fori_loop(lo, hi, pair, 0)
+
+
+def mid2(n, cg, hs_ref, b2_ref, dn2_ref, g_ref, db1_ref, gg_ref):
+    gg_ref[...] = jnp.zeros_like(gg_ref)
+    def body(r, o):
+        row = lax.broadcasted_iota(jnp.int32, (RB, 768), 0) + o
+        hs = hs_ref[r, :]
+        dy = cg[r, :].astype(f32)
+        cg[r, :] = jnp.where(row < n, hs + b2_ref[r, :], 0.0).astype(bf16)
+        inv = norm_block(hs, None)
+        dn = dn2_ref[r, :]
+        q = dn * g_ref[1:2, :]
+        gg_ref[1:2, :] += jnp.sum(hs * inv * dn, axis=0, keepdims=True)
+        dh = dy + (inv * q - hs * inv * inv * inv * jnp.mean(hs * q, axis=-1, keepdims=True))
+        hs_ref[r, :] = dh
+        db1_ref[r, :] = dh.astype(bf16)
+    rows_loop(hs_ref.shape[0], body)
+
+
+def all_kernel(nf, nd, perm, lens, tok, cot0, gm, am, fm, cos_ref, sin_ref,
+               oo, io, ggo, ao, fo,
+               xg, cg, cst, wa, wf, gt, gg, gains, ggb, gb, ggr,
+               n1, qkv, p0, p1, o, hs, n2, b2, dn2, gatt, gff,
+               arc, ar1, ar2, arz, frc, fr1, fr2, frz,
+               ss, rs, ls, ags, fgs, ass, fss, acs, a1s, a2s, azs, fcs, f1s, f2s, fzs):
+    t = Topo2(nf, nd)
+    N, Z = t.N, t.Z
+    L = xg.shape[0]; pos = L // N; ra = wa.shape[0] // N; gl = gm.shape[1]; R = wf.shape[2]
+    ps = (p0, p1)
+    row_at = lambda ref: (lambda z, g: ref.at[pl.ds(pl.multiple_of((z * 8 + g) * ra, ra), ra)])
+    blk_at = lambda ref: (lambda z, g: ref.at[z * 8 + g])
+    most = lambda ref: ref.at[pl.ds(0, L - pos)]
+    wa[pl.ds(pl.multiple_of(t.me * ra, ra), ra), :] = am[...].astype(bf16)
+    wf[t.me] = fm[...].astype(bf16)
+    gt[...] = jnp.zeros_like(gt)
+    gt[0:2, 0:gl] = gm[...].astype(bf16).astype(f32)
+    gg[t.me] = gt[...]
+    barrier_all(t)
+    A = Gather2(t, row_at(wa), ss.at[3], ags)
+    F = Gather2(t, blk_at(wf), ss.at[4], fgs)
+    tk = Exchange(t, lambda d: tok.at[d], rows_of(xg, pos), most(xg), most(xg), ss.at[0], rs.at[0], ls.at[0])
+    ct = Exchange(t, rows_of(cst, pos), rows_of(cg, pos), most(cg), most(cg), ss.at[1], rs.at[1], ls.at[1])
+    A.start()
+    tk.start()
+    def gs(k): rcopy(gt, gg.at[t.me], ss.at[2], rs.at[2], t.flat(lax.rem(t.me + k, N))).start()
+    loop(1, N, gs)
+    def pm(i): cst[pl.ds(pl.multiple_of(i * pos, pos), pos), :] = cot0[perm[i]]
+    loop(0, N, pm)
+    A.take(0, 1)
+    F.start()
+    A.take(1)
+    A.take(2); A.take(3)
+    F.take(0, 1)
+    for gi in range(4): A.take_sib(gi)
+    tk.wait_recv()
+    wait_bytes(gg.at[pl.ds(0, N - 1)], rs.at[2])
+    tot = jnp.zeros((8, 768), f32)
+    for d in range(N):
+        wide = jnp.concatenate([gg[d], jnp.zeros((8, 640), f32)], 1)
+        tot = tot + (pltpu.roll(wide, d * gl, 1) if d else wide)
+    gains[...] = tot
+    phase_norm1(xg, gains, n1)
+    phase_qkv(n1, wa, cos_ref, sin_ref, qkv)
+    F.take(1)
+    ct.start()
+    attn_fwd2(qkv, ps, o, 0, 3)
+    F.take(2)
+    attn_fwd2(qkv, ps, o, 3, 6)
+    phase_wo_norm2(o, wa, xg, gains, hs, n2)
+    F.take(3)
+    ct.wait_recv()
+    n = lens[t.me]
+    def mask(r, of):
+        row = lax.broadcasted_iota(jnp.int32, (RB, 768), 0) + of
+        cg[r, :] = jnp.where(row < n, cg[r, :].astype(f32), 0.0).astype(bf16)
+    rows_loop(L, mask)
+    SA = Scatter2(t, row_at(gatt), lambda z, g: gatt[pl.ds(pl.multiple_of((z * 8 + g) * ra, ra), ra), :], arc, ar1, ar2, arz, ass, acs, a1s, a2s, azs)
+    SF = Scatter2(t, blk_at(gff), lambda z, g: gff[z * 8 + g], frc, fr1, fr2, frz, fss, fcs, f1s, f2s, fzs)
+    def tile(i):
+        gi = i // 2
+        par = lax.rem(lax.rem(i, 2) + i // 6, 2)
+        cc = t.c + par * (1 - 2 * t.c)
+        g = t.g8(gi, cc)
+        @pl.when(par == 1)
+        def _(): F.take_sib(gi)
+        wg, wu, wd = (jnp.concatenate([wf[z * 8 + g, j] for z in range(Z)], 0) for j in range(3))
+        nv = n2[...]
+        ga = dot_nt(nv, wg); u = dot_nt(nv, wu)
+        da = dot_nt(cg[...], wd)
+        sg = 1.0 / (1.0 + jnp.exp2(ga * (-LOG2E)))
+        silu = ga * sg
+        a = (silu * u).astype(bf16)
+        dg = (da * u * (sg * (1.0 + ga * (1.0 - sg)))).astype(bf16)
+        du = (da * silu).astype(bf16)
+        bb = dot_nn(a, wd)
+        dn = dot_nn(dg, wg) + dot_nn(du, wu)
+        @pl.when(i == 0)
+        def _():
+            b2[...] = bb; dn2[...] = dn
+        @pl.when(i > 0)
+        def _():
+            b2[...] += bb; dn2[...] += dn
+        for j, (lhs, rhs) in enumerate(((dg, nv), (du, nv), (a, cg[...]))):
+            w = dot_tn(lhs, rhs).astype(bf16)
+            for z in range(Z): gff[z * 8 + g, j] = w[z * R:(z + 1) * R]
+        @pl.when(par == 1)
+        def _(): SF.start(gi)
+    loop(0, 8, tile)
+    mid2(n, cg, hs, b2, dn2, gains, n2, ggb)
+    ox = Exchange(t, rows_of(cg, pos), lambda d: oo.at[d], most(cg), oo.at[pl.ds(0, N - 1)], ss.at[5], rs.at[3], ls.at[3])
+    ix = Exchange(t, rows_of(n1, pos), lambda d: io.at[d], most(n1), io.at[pl.ds(0, N - 1)], ss.at[6], rs.at[4], ls.at[4])
+    SF.stage_c(3); SF.stage_c(2)
+    ox.start()
+    ct.wait_send()
+    phase_wo_back(n2, o, wa, cst, gatt)
+    SF.stage_c(1); SF.stage_c(0)
+    attn_bwd2(qkv, ps, cst, cos_ref, sin_ref, 0, 3)
+    SF.stage_1(0)
+    attn_bwd2(qkv, ps, cst, cos_ref, sin_ref, 3, 6)
+    phase_wqkv_grad(qkv, n1, gatt)
+    for gi in (3, 2, 1, 0): SA.start(gi)
+    SF.stage_1(1)
+    SF.stage_2()
+    SA.stage_c(3); SA.stage_c(2)
+    phase_dn1(qkv, wa, xg, gains, hs, n1, ggb)
+    ix.start()
+    for d in range(N):
+        v = ggb[...]
+        gb[d] = (pltpu.roll(v, 768 - d * gl, 1) if d else v)[:, 0:128]
+    ggr[t.me] = gb[t.me]
+    def gsend(k):
+        d = lax.rem(t.me + k, N)
+        rcopy(gb.at[d], ggr.at[t.me], ss.at[7], rs.at[5], t.flat(d)).start()
+    loop(1, N, gsend)
+    SA.stage_c(1); SA.stage_c(0)
+    SA.stage_1(0); SA.stage_1(1); SA.stage_2()
+    SF.final(fo)
+    wait_bytes(ggr.at[pl.ds(0, N - 1)], rs.at[5])
+    tot = ggr[0]
+    for d in range(1, N): tot = tot + ggr[d]
+    ggo[...] = tot
+    SA.final(ao)
+    ox.wait_recv(); ix.wait_recv()
+    tk.wait_send(); ox.wait_send(); ix.wait_send()
+    wait_bytes(gg.at[pl.ds(0, N - 1)], ss.at[2]); wait_bytes(ggr.at[pl.ds(0, N - 1)], ss.at[7])
+    wait_bytes(wa.at[pl.ds(0, (N - 1) * ra)], ss.at[3])
+    wait_bytes(wf.at[pl.ds(0, N - 1)], ss.at[4])
+    SF.wait_send(); SA.wait_send()
+
+
+def all_call(perm, lens, tok, cot, gm, am, fm, C, S):
+    nf, nd = lax.axis_size("fsdp"), lax.axis_size("dp"); N = nf * nd; Z = nf // 2
+    pos, D = tok.shape[1:]; L = pos * N; ra = am.shape[0]; R = fm.shape[1]
+    anyv = pl.BlockSpec(memory_space=pl.ANY); V = pl.BlockSpec(memory_space=pltpu.VMEM); SM = pl.BlockSpec(memory_space=pltpu.SMEM)
+    sd = jax.ShapeDtypeStruct; Q = pltpu.SemaphoreType.DMA
+    vm = lambda *s, dt=bf16: pltpu.VMEM(s, dt)
+    return pl.pallas_call(functools.partial(all_kernel, nf, nd),
+        out_shape=(sd(tok.shape, bf16), sd(tok.shape, bf16), sd((8, 128), f32), sd((ra, D), f32), sd((3, R, D), f32)),
+        in_specs=[SM, SM, anyv, V, V, V, V, V, V], out_specs=(anyv, anyv, V, V, V),
+        scratch_shapes=[vm(L, D), vm(L, D), vm(L, D), vm(N * ra, D), vm(N, 3, R, D), vm(8, 128, dt=f32), vm(N, 8, 128, dt=f32), vm(8, D, dt=f32),
+                        vm(8, D, dt=f32), vm(N, 8, 128, dt=f32), vm(N, 8, 128, dt=f32),
+                        vm(L, D), vm(L, 3 * D), vm(H, 256, 256), vm(H, 256, 512), vm(L, D), vm(L, D, dt=f32), vm(L, D), vm(L, D, dt=f32), vm(L, D, dt=f32),
+                        vm(N * ra, D), vm(N, 3, R, D)]
+                       + [vm(n, *sh) for sh in ((ra, D), (3, R, D)) for n in (4 * Z, 2 * Z, Z, Z - 1)]
+                       + [Q((8,)), Q((6,)), Q((5,)), Q((Z, 8)), Q((Z, 8)), Q((4,)), Q((4,))] + [Q((n,)) for _ in range(2) for n in (4 * Z, 2 * Z, Z, Z - 1)],
+        compiler_params=pltpu.CompilerParams(collective_id=2, has_side_effects=True, vmem_limit_bytes=64 * 2**20))(perm, lens, tok, cot, gm, am, fm, C, S)
+
+
+def update(w, q, m, v, decay, mo, vo, wo):
+    m2 = beta_first * m + (1.0 - beta_first) * q
+    v2 = beta_second * v + (1.0 - beta_second) * q * q
+    mo[...] = m2
+    vo[...] = v2
+    new = w - learning_rate * ((m2 / (1.0 - beta_first**STEP)) / (jnp.sqrt(v2 / (1.0 - beta_second**STEP)) + adam_epsilon) + decay * w)
+    wo[...] = new
+    return new
+
+
+def last_kernel(slot, oo, io, gs, ag, fg, am, amm, amv, fm, fmm, fmv, gm, gmm, gmv,
+                out, iout, ago, fgo, ggo, amo, avo, fmo, fvo, gmo, gvo, awo, fwo, gup, ac, fc):
+    N = oo.shape[0]; gl = gm.shape[1]
+    def pm(j): out[j] = oo[slot[j]]
+    loop(0, N, pm)
+    iout[...] = io[...]
+    ago[...] = ag[...]
+    fgo[...] = fg[...]
+    q = gs[0:2, 0:gl]
+    ggo[...] = q
+    ac[...] = update(am[...], ag[...], amm[...], amv[...], weight_decay, amo, avo, awo).astype(bf16)
+    fc[...] = update(fm[...], fg[...], fmm[...], fmv[...], weight_decay, fmo, fvo, fwo).astype(bf16)
+    w = gm[...]
+    gup[...] = update(w, q, gmm[...], gmv[...], 0.0, gmo, gvo, gup) - w
+
+
+def last_call(slot, oo, io, gs, ag, fg, am, amm, amv, fm, fmm, fmv, gm, gmm, gmv):
+    V = pl.BlockSpec(memory_space=pltpu.VMEM); SM = pl.BlockSpec(memory_space=pltpu.SMEM)
+    sd = lambda a, dt=None: jax.ShapeDtypeStruct(a.shape, dt or a.dtype)
+    return pl.pallas_call(last_kernel, in_specs=[SM] + [V] * 14, out_specs=(V,) * 16,
+        out_shape=(sd(oo), sd(io), sd(am), sd(fm), sd(gm), sd(am), sd(am), sd(fm), sd(fm), sd(gm), sd(gm), sd(am), sd(fm), sd(gm), sd(am, bf16), sd(fm, bf16)),
+        compiler_params=pltpu.CompilerParams(vmem_limit_bytes=48 * 2**20))(slot, oo, io, gs, ag, fg, am, amm, amv, fm, fmm, fmv, gm, gmm, gmv)
+
+
+def local_one(tokens, cotangent, lengths, device_sequence, slot_device, attention_master, feedforward_master, gains_master,
+              attention_mean, attention_square, feedforward_mean, feedforward_square, gains_mean, gains_square):
+    N = lax.axis_size(AX)
+    counter = jnp.arange(N, dtype=jnp.int32)
+    slot_sequence = jnp.sum(jnp.where(slot_device[:, None] == counter[None, :], device_sequence[None, :], 0), axis=1)
+    slot_of_sequence = jnp.sum(jnp.where(slot_sequence[:, None] == counter[None, :], counter[:, None], 0), axis=0)
+    tr = lambda a: a.transpose(1, 0, 2)
+    C, S = tables(tokens.shape[1] * N)
+    oo, io, gs, ag, fg = all_call(slot_of_sequence, lengths, tokens, cotangent, gains_master, attention_master, tr(feedforward_master), jnp.asarray(C), jnp.asarray(S))
+    r = list(last_call(slot_sequence, oo, io, gs, ag, fg, attention_master, attention_mean, attention_square,
+                       tr(feedforward_master), tr(feedforward_mean), tr(feedforward_square), gains_master, gains_mean, gains_square))
+    for i in (3, 7, 8, 12, 15): r[i] = tr(r[i])
+    return tuple(r)
+
+
 def solution(mesh):
     t, r, f, g = P(None, AX, None), P(AX, None), P(AX, None, None), P(None, AX)
     in_specs = (t, t, P(), P(), P(), r, f, g, r, r, f, f, g, g)
     out_specs = (t, t, r, f, g, r, r, f, f, g, g, r, f, g, r, f)
-    return jax.shard_map(local, mesh=mesh, in_specs=in_specs, out_specs=out_specs, check_vma=False)
+    n = mesh.shape["fsdp"] * mesh.shape["dp"]
+    body = local_one if 512 // n % 16 == 0 and 3072 // n % 16 == 0 else local
+    return jax.shard_map(body, mesh=mesh, in_specs=in_specs, out_specs=out_specs, check_vma=False)

time: 306 us -> 254 us (0.83)
  Pallas kernels: 282 us -> 238 us
  other arithmetic: 13.5 us -> 0.78 us
  local copies, waits for them, and re-layouts: 9.02 us -> 12.2 us
    pallas_call x3 -> x2, Pallas kernels: 282 us -> 238 us  [the longest x1 234 us: all_call(): pl.pallas_call(functools.partial(all_kernel, nf, nd), out_shape=(sd(tok.s...]
    convert_element_type x5 -> x0, other arithmetic: 8.87 us -> none  [the longest x1 2.68 us: local(): master_feedforward.astype(bf16)]
    unnamed x28 -> x36, local copies, waits for them, and re-layouts: 5.72 us -> 12.2 us
where the time goes in v2:
time: 254 us; the launch traced here: 252 us
  Pallas kernels  238 us (94%)
  local copies, waits for them, and re-layouts  12.2 us (5%)
    pallas_call x1, Pallas kernels, all_call(): pl.pallas_call(functools.partial(all_kernel, nf, nd), out_shape=(sd(tok.s...  234 us
    unnamed x36, local copies, waits for them, and re-layouts  12.2 us

profile of v2, /device:TPU:8, one launch (start us, length us, event | category | flops | bytes accessed | tf_op | source)
XLA Modules:
  0.0 251.7 jit_solution(9501000995195556761)
XLA Ops:
  0.6 0.0 copy-start.16
  0.7 0.0 copy-start.17
  0.7 0.6 copy-done.16
  1.3 0.0 copy-done.17
  1.3 0.2 select_reduce_fusion.1.slot
  1.5 0.6 select_reduce_fusion.perm
  2.1 0.0 copy-start.14
  2.1 0.5 copy-done.14
  2.6 234.3 %shard_map.279 = (bf16[32,16,768]{2,1,0:T(8,128)(2,1)}, bf16[32,16,768]{2,1,0:T(8,128)(2,1)}, f32[8,128]{1,0:T(8,128)}, f32[96,768]{1,0:T(8,128)}, f32[3,64,768]{2,1,0:T(8,128)}) custom-call(s32[32]{0:T(128)} %select_reduce_fusion.perm, s32[32]{0:T(128)} %lens.1, bf16[32,16,768]{2,1,0:T(8,128)(2,1)} %tok.1, bf16[32,16,768]{2,1,0:T(8,128)(2,1)} %cot0.1, ...), custom_call_target="tpu_custom_call" | custom-call | tf_op jit(solution)/shard_map/pallas_call | solution.py:838
  236.9 0.0 copy-start.11
  236.9 0.0 copy-start.12
  236.9 0.0 copy-start.13
  236.9 0.0 copy-start.10
  237.0 0.0 copy-start.15
  237.0 0.6 copy-done.11
  237.6 0.0 copy-done.12
  237.6 0.0 copy-done.13
  237.6 0.0 copy-done.10
  237.6 0.0 copy-done.15
  237.6 0.0 copy-start
  237.6 1.1 copy-done
  238.7 0.0 copy-start.1
  238.7 1.0 copy-done.1
  239.7 0.0 copy-start.2
  239.7 1.1 copy-done.2
  240.8 0.0 copy-start.3
  240.8 1.1 copy-done.3
  241.9 0.0 copy-start.4
  241.9 1.1 copy-done.4
  243.0 0.0 copy-start.5
  243.0 1.1 copy-done.5
  244.1 0.0 copy-start.6
  244.1 1.1 copy-done.6
  245.1 0.0 copy-start.7
  245.1 1.0 copy-done.7
  246.1 0.0 copy-start.8
  246.1 1.0 copy-done.8
  247.1 0.0 copy-start.9
  247.1 1.0 copy-done.9
  248.0 3.7 %shard_map.280 = (bf16[32,16,768]{2,1,0:T(8,128)(2,1)}, bf16[32,16,768]{2,1,0:T(8,128)(2,1)}, f32[96,768]{1,0:T(8,128)}, f32[3,64,768]{2,1,0:T(8,128)}, f32[2,24...) custom-call(s32[32]{0:T(128)S(1)} %copy-done.15, ...), custom_call_target="tpu_custom_call" | custom-call | tf_op jit(solution)/shard_map/pallas_call | solution.py:879
Async XLA Ops:
  0.6 0.7 copy-start.16
  0.7 0.7 copy-start.17
  2.1 0.5 copy-start.14
  236.9 0.7 copy-start.11
  236.9 0.7 copy-start.12
  236.9 0.7 copy-start.13
  236.9 0.7 copy-start.10
  237.0 0.7 copy-start.15
  237.6 1.1 copy-start
  238.7 1.0 copy-start.1
  239.7 1.1 copy-start.2
  240.8 1.1 copy-start.3
  241.9 1.1 copy-start.4
  243.0 1.1 copy-start.5
  244.1 1.1 copy-start.6
  245.1 1.0 copy-start.7
  246.1 1.0 copy-start.8
  247.1 1.0 copy-start.9

commit v3 on v2

--- a/solution.py
+++ b/solution.py
@@ -539,81 +539,136 @@
 
 
 class Gather2:
-    def __init__(s, t, at, ssem, rsem): s.t, s.at, s.ssem, s.rsem = t, at, ssem, rsem
+    def __init__(s, t, at, ssem, zsem, rsem): s.t, s.at, s.ssem, s.zsem, s.rsem = t, at, ssem, zsem, rsem
     def send(s, z, g, dev):
         rcopy(s.at(z, g), s.at(z, g), s.ssem, s.rsem.at[z, g], dev).start()
     def wait(s, z, g): wait_bytes(s.at(z, g), s.rsem.at[z, g])
+    def along(s, z, g, side, f):
+        t = s.t
+        @pl.when((t.z + side >= 0) & (t.z + side < t.Z))
+        def _(): f(rcopy(s.at(z, g), s.at(z, g), s.zsem.at[z, (side + 1) // 2], s.rsem.at[z, g], t.dev(t.z + side, t.y, t.x, t.c)))
     def start(s):
         t = s.t; g = t.g8(0, t.c)
-        loop(1, t.Z, lambda k: s.send(t.z, g, t.dev(t.zk(k), t.y, t.x, t.c)))
+        for side in (-1, 1): s.along(t.z, g, side, lambda c: c.start())
         for dev in (t.p1, t.p2, t.sib): s.send(t.z, g, dev)
+    def sweep(s, lo, hi, f):
+        t = s.t
+        def step(j):
+            @pl.when(t.z - j >= 0)
+            def _(): f(t.z - j, -1)
+            @pl.when(t.z + j < t.Z)
+            def _(): f(t.z + j, 1)
+        if lo == 0: f(t.z, 0)
+        loop(max(lo, 1), hi, step)
     def take(s, gi, lo=0, hi=None):
         t = s.t; g = t.g8(gi, t.c)
         to = {0: (t.p1, t.p2, t.sib), 1: (t.p2, t.sib)}.get(gi, (t.sib,))
-        def f(k):
-            z = t.zk(k); s.wait(z, g)
+        def f(z, side):
+            s.wait(z, g)
+            if gi == 0: s.along(z, g, -side, lambda c: c.start())
             for dev in to: s.send(z, g, dev)
-        loop(lo, t.Z if hi is None else hi, f)
-    def take_sib(s, gi):
+        s.sweep(lo, t.Z if hi is None else hi, f)
+    def take_sib(s, gi, lo=0, hi=None):
         t = s.t; g = t.g8(gi, t.cb)
-        loop(0, t.Z, lambda k: s.wait(t.zk(k), g))
-
-
-class Scatter2:
-    def __init__(s, t, at, ld, rc, r1, r2, rz, ss, rcs, r1s, r2s, rzs):
-        s.t, s.at, s.ld, s.rc, s.r1, s.r2, s.rz, s.ss, s.rcs, s.r1s, s.r2s, s.rzs = t, at, ld, rc, r1, r2, rz, ss, rcs, r1s, r2s, rzs
-        s.Z = t.Z
+        s.sweep(lo, t.Z if hi is None else hi, lambda z, side: s.wait(z, g))
+    def finish(s, bulk):
+        t = s.t; g = t.g8(0, t.c)
+        wait_bytes(bulk, s.ssem)
+        for side in (-1, 1): s.along(t.z, g, side, lambda c: c.wait_send())
+        s.sweep(1, t.Z, lambda z, side: s.along(z, g, -side, lambda c: c.wait_send()))
+
+
+SEQ = ((0, 1), (1, 0), (0, 2), (1, 1), (2, 0), (0, 3), (1, 2), (2, 1), (3, 0), (1, 3), (2, 2), (3, 1), (2, 3), (3, 2), (3, 3))
+
+
+class Scatter3:
+    def __init__(s, t, at, ld, rc, r1, r2, rz, ss, rcs, r1s, r2s, rzs, zss):
+        s.t, s.at, s.ld, s.rc, s.r1, s.r2, s.rz, s.ss, s.rcs, s.r1s, s.r2s, s.rzs, s.zss = t, at, ld, rc, r1, r2, rz, ss, rcs, r1s, r2s, rzs, zss
+        s.Z = Z = t.Z
+        s.order = [sorted(range(Z), key=lambda q: (-abs(q - z), (q > z) == (z < Z // 2))) for z in range(Z)]
+    def zof(s, i):
+        r = 0
+        for z in range(s.Z): r = r + jnp.where(s.t.z == z, s.order[z][i], 0)
+        return r
     def start(s, gi):
         t = s.t; Z = s.Z; g = t.g8(gi, t.cb)
-        def f(k):
-            j = (3 - gi) * Z + k
-            rcopy(s.at(t.zk(k), g), s.rc.at[j], s.ss.at[0], s.rcs.at[j], t.sib).start()
-        loop(0, Z, f)
-    def stage_c(s, gi):
-        t = s.t; Z = s.Z; g = t.g8(gi, t.c)
-        def f(k):
-            j = (3 - gi) * Z + k
+        for i in range(Z):
+            z = s.zof(i); j = (3 - gi) * Z + z
+            rcopy(s.at(z, g), s.rc.at[j], s.ss.at[0], s.rcs.at[j], t.sib).start()
+    def chip(s, z, gs):
+        t = s.t; Z = s.Z
+        for gi in gs:
+            j = (3 - gi) * Z + z
             wait_bytes(s.rc.at[j], s.rcs.at[j])
-            s.rc[j] = s.rc[j] + s.ld(t.zk(k), g)
+            s.rc[j] = s.rc[j] + s.ld(z, t.g8(gi, t.c))
             if gi >= 2: rcopy(s.rc.at[j], s.r1.at[j], s.ss.at[1], s.r1s.at[j], t.p2).start()
-        loop(0, Z, f)
-    def stage_1(s, h):
+    def first(s, z):
         t = s.t; Z = s.Z
-        def f(k):
-            j = h * Z + k
+        for h in range(2):
+            j = h * Z + z
             wait_bytes(s.r1.at[j], s.r1s.at[j])
             s.r1[j] = s.r1[j] + s.rc[2 * Z + j]
-            if h == 0: rcopy(s.r1.at[j], s.r2.at[k], s.ss.at[2], s.r2s.at[k], t.p1).start()
+            if h == 0: rcopy(s.r1.at[z], s.r2.at[z], s.ss.at[2], s.r2s.at[z], t.p1).start()
+    def hop(s, z, side):
+        t = s.t
+        j = jnp.where((z == t.z + side) & (side < 0), s.Z, z)
+        return rcopy(s.r2.at[z], s.rz.at[j], s.zss.at[z], s.rzs.at[j], t.dev(t.z + side, t.y, t.x, t.c))
+    def second(s, z):
+        t = s.t; Z = s.Z
+        wait_bytes(s.r2.at[z], s.r2s.at[z])
+        s.r2[z] = s.r2[z] + s.r1[Z + z]
+    def line(s, z):
+        t = s.t; Z = s.Z
+        for side in (-1, 1):
+            @pl.when((z - t.z) * side > 0)
+            def _():
+                @pl.when((t.z - side >= 0) & (t.z - side < Z))
+                def _():
+                    wait_bytes(s.rz.at[z], s.rzs.at[z])
+                    s.r2[z] = s.r2[z] + s.rz[z]
+                s.hop(z, side).start()
+    def C(s, *ii):
+        for i in ii: s.chip(s.zof(i), (3, 2, 1, 0))
+    def F(s, *ii):
+        for i in ii: s.first(s.zof(i))
+    def S(s, *ii):
+        for i in ii: s.second(s.zof(i)); s.line(s.zof(i))
+    def total(s):
+        t = s.t; Z = s.Z
+        tot = s.r2[t.z].astype(f32)
+        below = jnp.where(t.z > 0, 1.0, 0.0); above = jnp.where(t.z < Z - 1, 1.0, 0.0)
+        @pl.when(t.z > 0)
+        def _(): wait_bytes(s.rz.at[t.z], s.rzs.at[t.z])
+        @pl.when(t.z == 0)
+        def _(): s.rz[t.z] = jnp.zeros(s.rz.shape[1:], bf16)
+        @pl.when(t.z < Z - 1)
+        def _(): wait_bytes(s.rz.at[Z], s.rzs.at[Z])
+        @pl.when(t.z == Z - 1)
+        def _(): s.rz[Z] = jnp.zeros(s.rz.shape[1:], bf16)
+        return tot + (s.rz[t.z].astype(f32) + s.rz[Z].astype(f32))
+    def wait_send(s):
+        t = s.t; Z = s.Z
+        wait_bytes(s.rc, s.ss.at[0]); wait_bytes(s.r1, s.ss.at[1]); wait_bytes(s.r2, s.ss.at[2])
+        def f(z):
+            for side in (-1, 1):
+                @pl.when((z - t.z) * side > 0)
+                def _(): s.hop(z, side).wait_send()
         loop(0, Z, f)
-    def stage_2(s):
-        t = s.t; Z = s.Z
-        def f(k):
-            wait_bytes(s.r2.at[k], s.r2s.at[k])
-            s.r2[k] = s.r2[k] + s.r1[Z + k]
-            rcopy(s.r2.at[k], s.rz.at[Z - k - 1], s.ss.at[3], s.rzs.at[Z - k - 1], t.dev(t.zk(k), t.y, t.x, t.c)).start()
-        loop(1, Z, f)
-        wait_bytes(s.r2.at[0], s.r2s.at[0])
-    def final(s, out):
-        Z = s.Z
-        tot = s.r2[0].astype(f32) + s.r1[Z].astype(f32)
-        for k in range(Z - 1):
-            wait_bytes(s.rz.at[k], s.rzs.at[k])
-            tot = tot + s.rz[k].astype(f32)
-        out[...] = tot
-    def wait_send(s):
-        wait_bytes(s.rc, s.ss.at[0]); wait_bytes(s.r1, s.ss.at[1]); wait_bytes(s.r2, s.ss.at[2]); wait_bytes(s.rz, s.ss.at[3])
 
 
 class Exchange:
     def __init__(s, t, src, dst, sbulk, dbulk, ssem, rsem, lsem):
         s.t, s.src, s.dst, s.sbulk, s.dbulk, s.ssem, s.rsem, s.lsem = t, src, dst, sbulk, dbulk, ssem, rsem, lsem
-    def start(s):
+        s.sent = 1
+    def start(s): pltpu.make_async_copy(s.src(s.t.me), s.dst(s.t.me), s.lsem).start()
+    def more(s, n):
         t = s.t
-        pltpu.make_async_copy(s.src(t.me), s.dst(t.me), s.lsem).start()
         def f(k):
             d = lax.rem(t.me + k, t.N)
             rcopy(s.src(d), s.dst(t.me), s.ssem, s.rsem, t.flat(d)).start()
-        loop(1, t.N, f)
+        to = min(t.N, s.sent + n)
+        if to > s.sent: loop(s.sent, to, f)
+        s.sent = to
     def wait_recv(s):
         pltpu.make_async_copy(s.src(s.t.me), s.dst(s.t.me), s.lsem).wait()
         wait_bytes(s.dbulk, s.rsem)
@@ -644,7 +699,8 @@
                 pr = (e * (1.0 / jnp.sum(e, axis=-1, keepdims=True))).astype(bf16)
                 ps[i][2 * t + h] = pr
                 got.append(pr)
-            o_ref[i * QB:kl, pl.ds(oq, 128)] = dot_nn(jnp.concatenate(got, 1), jnp.concatenate(v, 0)).astype(bf16)
+            n = o_ref.shape[1]
+            o_ref[i * QB // n:kl // n, :, pl.ds(oq, 128)] = dot_nn(jnp.concatenate(got, 1), jnp.concatenate(v, 0)).astype(bf16).reshape(QB // n, n, 128)
         return carry
     lax.fori_loop(lo, hi, pair, 0)
 
@@ -681,6 +737,26 @@
     lax.fori_loop(lo, hi, pair, 0)
 
 
+def wo_norm2(o_ref, w_ref, x_ref, g_ref, hs_ref, n2_ref):
+    L = x_ref.shape[0]; R = 128; n = o_ref.shape[1]
+    def it(i, carry):
+        r = pl.ds(pl.multiple_of(i * R, R), R)
+        hs = x_ref[r, :].astype(f32) + dot_nn(o_ref[pl.ds(i * (R // n), R // n)].reshape(R, 768), w_ref[2304:3072, :])
+        hs_ref[r, :] = hs
+        n2_ref[r, :] = (hs * norm_block(hs, None) * g_ref[1:2, :]).astype(bf16)
+        return carry
+    lax.fori_loop(0, L // R, it, 0)
+
+
+def wo_back2(db1_ref, o_ref, w_ref, do_ref, gatt_ref):
+    def it(n, carry):
+        o = pl.multiple_of(n * 256, 256); w = pl.ds(pl.multiple_of(2304 + o, 256), 256)
+        do_ref[:, pl.ds(o, 256)] = dot_nt(db1_ref[...], w_ref[w, :]).astype(bf16)
+        gatt_ref[w, :] = dot_tn(o_ref[:, :, pl.ds(o, 256)].reshape(-1, 256), db1_ref[...]).astype(bf16)
+        return carry
+    lax.fori_loop(0, 3, it, 0)
+
+
 def mid2(n, cg, hs_ref, b2_ref, dn2_ref, g_ref, db1_ref, gg_ref):
     gg_ref[...] = jnp.zeros_like(gg_ref)
     def body(r, o):
@@ -701,9 +777,9 @@
 def all_kernel(nf, nd, perm, lens, tok, cot0, gm, am, fm, cos_ref, sin_ref,
                oo, io, ggo, ao, fo,
                xg, cg, cst, wa, wf, gt, gg, gains, ggb, gb, ggr,
-               n1, qkv, p0, p1, o, hs, n2, b2, dn2, gatt, gff,
+               n1, qkv, p0, p1, o, hs, n2, b2, dn2, gatt, gff, cs, sn,
                arc, ar1, ar2, arz, frc, fr1, fr2, frz,
-               ss, rs, ls, ags, fgs, ass, fss, acs, a1s, a2s, azs, fcs, f1s, f2s, fzs):
+               ss, rs, ls, azs2, fzs2, ags, fgs, ass, fss, acs, a1s, a2s, azs, azq, fcs, f1s, f2s, fzs, fzq):
     t = Topo2(nf, nd)
     N, Z = t.N, t.Z
     L = xg.shape[0]; pos = L // N; ra = wa.shape[0] // N; gl = gm.shape[1]; R = wf.shape[2]
@@ -711,27 +787,38 @@
     row_at = lambda ref: (lambda z, g: ref.at[pl.ds(pl.multiple_of((z * 8 + g) * ra, ra), ra)])
     blk_at = lambda ref: (lambda z, g: ref.at[z * 8 + g])
     most = lambda ref: ref.at[pl.ds(0, L - pos)]
-    wa[pl.ds(pl.multiple_of(t.me * ra, ra), ra), :] = am[...].astype(bf16)
-    wf[t.me] = fm[...].astype(bf16)
+    f0 = b2.at[pl.ds(0, ra)], dn2.at[pl.ds(0, 3 * R)]
+    near = [pltpu.make_async_copy(a, d, ls.at[5 + i]) for i, (a, d) in enumerate(((am, f0[0]), (fm, f0[1]), (cot0, o), (cos_ref, cs), (sin_ref, sn)))]
+    for c in near: c.start()
+    near[0].wait()
+    wa[pl.ds(pl.multiple_of(t.me * ra, ra), ra), :] = f0[0][...].astype(bf16)
+    near[1].wait()
+    wf[t.me] = f0[1][...].astype(bf16).reshape(3, R, 768)
     gt[...] = jnp.zeros_like(gt)
     gt[0:2, 0:gl] = gm[...].astype(bf16).astype(f32)
     gg[t.me] = gt[...]
     barrier_all(t)
-    A = Gather2(t, row_at(wa), ss.at[3], ags)
-    F = Gather2(t, blk_at(wf), ss.at[4], fgs)
+    A = Gather2(t, row_at(wa), ss.at[3], azs2, ags)
+    F = Gather2(t, blk_at(wf), ss.at[4], fzs2, fgs)
     tk = Exchange(t, lambda d: tok.at[d], rows_of(xg, pos), most(xg), most(xg), ss.at[0], rs.at[0], ls.at[0])
     ct = Exchange(t, rows_of(cst, pos), rows_of(cg, pos), most(cg), most(cg), ss.at[1], rs.at[1], ls.at[1])
+    def takes(X, lo, hi, *more):
+        for g, d in SEQ[lo:hi]:
+            X.take(g, d, d + 1)
+            for e, k in more: e.more(k)
+    tk.start()
     A.start()
-    tk.start()
+    tk.more(8)
+    takes(A, 0, 3, (tk, 3))
+    F.start()
+    near[2].wait()
+    def pm(i): cst[pl.ds(pl.multiple_of(i * pos, pos), pos), :] = o[perm[i]]
+    loop(0, N, pm)
+    ct.start()
     def gs(k): rcopy(gt, gg.at[t.me], ss.at[2], rs.at[2], t.flat(lax.rem(t.me + k, N))).start()
     loop(1, N, gs)
-    def pm(i): cst[pl.ds(pl.multiple_of(i * pos, pos), pos), :] = cot0[perm[i]]
-    loop(0, N, pm)
-    A.take(0, 1)
-    F.start()
-    A.take(1)
-    A.take(2); A.take(3)
-    F.take(0, 1)
+    takes(A, 3, 15, (tk, 3))
+    tk.more(N)
     for gi in range(4): A.take_sib(gi)
     tk.wait_recv()
     wait_bytes(gg.at[pl.ds(0, N - 1)], rs.at[2])
@@ -740,28 +827,38 @@
         wide = jnp.concatenate([gg[d], jnp.zeros((8, 640), f32)], 1)
         tot = tot + (pltpu.roll(wide, d * gl, 1) if d else wide)
     gains[...] = tot
+    takes(F, 0, 2, (ct, 3))
     phase_norm1(xg, gains, n1)
-    phase_qkv(n1, wa, cos_ref, sin_ref, qkv)
-    F.take(1)
-    ct.start()
-    attn_fwd2(qkv, ps, o, 0, 3)
-    F.take(2)
-    attn_fwd2(qkv, ps, o, 3, 6)
-    phase_wo_norm2(o, wa, xg, gains, hs, n2)
-    F.take(3)
+    takes(F, 2, 4, (ct, 3))
+    near[3].wait(); near[4].wait()
+    phase_qkv(n1, wa, cs, sn, qkv)
+    takes(F, 4, 6, (ct, 4))
+    def fwd(i):
+        attn_fwd2(qkv, ps, o, i, i + 1)
+    loop(0, 2, fwd)
+    takes(F, 6, 8, (ct, 4))
+    loop(2, 4, fwd)
+    takes(F, 8, 10, (ct, 4))
+    loop(4, 6, fwd)
+    ct.more(N)
+    wo_norm2(o, wa, xg, gains, hs, n2)
+    takes(F, 10, 11)
     ct.wait_recv()
     n = lens[t.me]
     def mask(r, of):
         row = lax.broadcasted_iota(jnp.int32, (RB, 768), 0) + of
         cg[r, :] = jnp.where(row < n, cg[r, :].astype(f32), 0.0).astype(bf16)
     rows_loop(L, mask)
-    SA = Scatter2(t, row_at(gatt), lambda z, g: gatt[pl.ds(pl.multiple_of((z * 8 + g) * ra, ra), ra), :], arc, ar1, ar2, arz, ass, acs, a1s, a2s, azs)
-    SF = Scatter2(t, blk_at(gff), lambda z, g: gff[z * 8 + g], frc, fr1, fr2, frz, fss, fcs, f1s, f2s, fzs)
+    SA = Scatter3(t, row_at(gatt), lambda z, g: gatt[pl.ds(pl.multiple_of((z * 8 + g) * ra, ra), ra), :], arc, ar1, ar2, arz, ass, acs, a1s, a2s, azs, azq)
+    SF = Scatter3(t, blk_at(gff), lambda z, g: gff[z * 8 + g], frc, fr1, fr2, frz, fss, fcs, f1s, f2s, fzs, fzq)
     def tile(i):
         gi = i // 2
         par = lax.rem(lax.rem(i, 2) + i // 6, 2)
         cc = t.c + par * (1 - 2 * t.c)
         g = t.g8(gi, cc)
+        for k, lo, hi in ((1, 11, 12), (2, 12, 13), (3, 13, 14), (4, 14, 15)):
+            @pl.when(i == k)
+            def _(): takes(F, lo, hi)
         @pl.when(par == 1)
         def _(): F.take_sib(gi)
         wg, wu, wd = (jnp.concatenate([wf[z * 8 + g, j] for z in range(Z)], 0) for j in range(3))
@@ -787,24 +884,27 @@
         @pl.when(par == 1)
         def _(): SF.start(gi)
     loop(0, 8, tile)
-    mid2(n, cg, hs, b2, dn2, gains, n2, ggb)
     ox = Exchange(t, rows_of(cg, pos), lambda d: oo.at[d], most(cg), oo.at[pl.ds(0, N - 1)], ss.at[5], rs.at[3], ls.at[3])
     ix = Exchange(t, rows_of(n1, pos), lambda d: io.at[d], most(n1), io.at[pl.ds(0, N - 1)], ss.at[6], rs.at[4], ls.at[4])
-    SF.stage_c(3); SF.stage_c(2)
-    ox.start()
+    SF.C(0, 1)
+    mid2(n, cg, hs, b2, dn2, gains, n2, ggb)
+    ox.start(); ox.more(8)
     ct.wait_send()
-    phase_wo_back(n2, o, wa, cst, gatt)
-    SF.stage_c(1); SF.stage_c(0)
-    attn_bwd2(qkv, ps, cst, cos_ref, sin_ref, 0, 3)
-    SF.stage_1(0)
-    attn_bwd2(qkv, ps, cst, cos_ref, sin_ref, 3, 6)
+    wo_back2(n2, o, wa, cst, gatt)
+    ox.more(8)
+    def back(i):
+        attn_bwd2(qkv, ps, cst, cs, sn, i, i + 1)
+    loop(0, 1, back)
+    SF.F(0); SF.C(2); ox.more(8)
+    loop(1, 4, back)
+    SF.F(1); SF.S(0); SF.C(3); ox.more(N)
+    loop(4, 6, back)
     phase_wqkv_grad(qkv, n1, gatt)
     for gi in (3, 2, 1, 0): SA.start(gi)
-    SF.stage_1(1)
-    SF.stage_2()
-    SA.stage_c(3); SA.stage_c(2)
+    SF.F(2); SF.S(1)
     phase_dn1(qkv, wa, xg, gains, hs, n1, ggb)
-    ix.start()
+    SA.C(0, 1)
+    ix.start(); ix.more(8)
     for d in range(N):
         v = ggb[...]
         gb[d] = (pltpu.roll(v, 768 - d * gl, 1) if d else v)[:, 0:128]
@@ -813,37 +913,45 @@
         d = lax.rem(t.me + k, N)
         rcopy(gb.at[d], ggr.at[t.me], ss.at[7], rs.at[5], t.flat(d)).start()
     loop(1, N, gsend)
-    SA.stage_c(1); SA.stage_c(0)
-    SA.stage_1(0); SA.stage_1(1); SA.stage_2()
-    SF.final(fo)
+    SF.F(3); SF.S(2)
+    SA.F(0); SA.C(2); ix.more(8)
+    SF.S(3)
+    SA.F(1); SA.S(0); SA.C(3); ix.more(N)
+    SA.F(2); SA.S(1)
+    f0[1][...] = SF.total().reshape(3 * R, 768)
+    far = [pltpu.make_async_copy(f0[1], fo, ls.at[6]), pltpu.make_async_copy(f0[0], ao, ls.at[5])]
+    far[0].start()
+    SA.F(3); SA.S(2); SA.S(3)
     wait_bytes(ggr.at[pl.ds(0, N - 1)], rs.at[5])
     tot = ggr[0]
     for d in range(1, N): tot = tot + ggr[d]
     ggo[...] = tot
-    SA.final(ao)
+    f0[0][...] = SA.total()
+    far[1].start()
     ox.wait_recv(); ix.wait_recv()
+    for c in far: c.wait()
     tk.wait_send(); ox.wait_send(); ix.wait_send()
     wait_bytes(gg.at[pl.ds(0, N - 1)], ss.at[2]); wait_bytes(ggr.at[pl.ds(0, N - 1)], ss.at[7])
-    wait_bytes(wa.at[pl.ds(0, (N - 1) * ra)], ss.at[3])
-    wait_bytes(wf.at[pl.ds(0, N - 1)], ss.at[4])
+    A.finish(wa.at[pl.ds(0, 7 * Z * ra)])
+    F.finish(wf.at[pl.ds(0, 7 * Z)])
     SF.wait_send(); SA.wait_send()
 
 
 def all_call(perm, lens, tok, cot, gm, am, fm, C, S):
     nf, nd = lax.axis_size("fsdp"), lax.axis_size("dp"); N = nf * nd; Z = nf // 2
-    pos, D = tok.shape[1:]; L = pos * N; ra = am.shape[0]; R = fm.shape[1]
-    anyv = pl.BlockSpec(memory_space=pl.ANY); V = pl.BlockSpec(memory_space=pltpu.VMEM); SM = pl.BlockSpec(memory_space=pltpu.SMEM)
+    pos, D = tok.shape[1:]; L = pos * N; ra = am.shape[0]; R = fm.shape[0] // 3
+    hbm = pl.BlockSpec(memory_space=pltpu.HBM); V = pl.BlockSpec(memory_space=pltpu.VMEM); SM = pl.BlockSpec(memory_space=pltpu.SMEM)
     sd = jax.ShapeDtypeStruct; Q = pltpu.SemaphoreType.DMA
     vm = lambda *s, dt=bf16: pltpu.VMEM(s, dt)
     return pl.pallas_call(functools.partial(all_kernel, nf, nd),
-        out_shape=(sd(tok.shape, bf16), sd(tok.shape, bf16), sd((8, 128), f32), sd((ra, D), f32), sd((3, R, D), f32)),
-        in_specs=[SM, SM, anyv, V, V, V, V, V, V], out_specs=(anyv, anyv, V, V, V),
+        out_shape=(sd(tok.shape, bf16), sd(tok.shape, bf16), sd((8, 128), f32), sd((ra, D), f32), sd((3 * R, D), f32)),
+        in_specs=[SM, SM, hbm, hbm, V, hbm, hbm, hbm, hbm], out_specs=(hbm, hbm, V, hbm, hbm),
         scratch_shapes=[vm(L, D), vm(L, D), vm(L, D), vm(N * ra, D), vm(N, 3, R, D), vm(8, 128, dt=f32), vm(N, 8, 128, dt=f32), vm(8, D, dt=f32),
                         vm(8, D, dt=f32), vm(N, 8, 128, dt=f32), vm(N, 8, 128, dt=f32),
-                        vm(L, D), vm(L, 3 * D), vm(H, 256, 256), vm(H, 256, 512), vm(L, D), vm(L, D, dt=f32), vm(L, D), vm(L, D, dt=f32), vm(L, D, dt=f32),
-                        vm(N * ra, D), vm(N, 3, R, D)]
-                       + [vm(n, *sh) for sh in ((ra, D), (3, R, D)) for n in (4 * Z, 2 * Z, Z, Z - 1)]
-                       + [Q((8,)), Q((6,)), Q((5,)), Q((Z, 8)), Q((Z, 8)), Q((4,)), Q((4,))] + [Q((n,)) for _ in range(2) for n in (4 * Z, 2 * Z, Z, Z - 1)],
+                        vm(L, D), vm(L, 3 * D), vm(H, 256, 256), vm(H, 256, 512), vm(N, pos, D), vm(L, D, dt=f32), vm(L, D), vm(L, D, dt=f32), vm(L, D, dt=f32),
+                        vm(N * ra, D), vm(N, 3, R, D), vm(L, 128, dt=f32), vm(L, 128, dt=f32)]
+                       + [vm(n, *sh) for sh in ((ra, D), (3, R, D)) for n in (4 * Z, 2 * Z, Z, Z + 1)]
+                       + [Q((8,)), Q((6,)), Q((10,)), Q((Z, 2)), Q((Z, 2)), Q((Z, 8)), Q((Z, 8)), Q((4,)), Q((4,))] + [Q((n,)) for _ in range(2) for n in (4 * Z, 2 * Z, Z, Z + 1, Z)],
         compiler_params=pltpu.CompilerParams(collective_id=2, has_side_effects=True, vmem_limit_bytes=64 * 2**20))(perm, lens, tok, cot, gm, am, fm, C, S)
 
 
@@ -857,28 +965,51 @@
     return new
 
 
-def last_kernel(slot, oo, io, gs, ag, fg, am, amm, amv, fm, fmm, fmv, gm, gmm, gmv,
-                out, iout, ago, fgo, ggo, amo, avo, fmo, fvo, gmo, gvo, awo, fwo, gup, ac, fc):
-    N = oo.shape[0]; gl = gm.shape[1]
-    def pm(j): out[j] = oo[slot[j]]
+def last_kernel(slot, *refs):
+    ins, outs, iv, ov, isem, osem = refs[:14], refs[14:30], refs[30:44], refs[44:57], refs[57], refs[58]
+    oo, io, gs, ag, fg = ins[:5]
+    N = oo.shape[0]; gl = ins[11].shape[1]
+    order = [8, 9, 10, 4, 5, 6, 7, 3, 1, 11, 12, 13, 2, 0]
+    src = {k: pltpu.make_async_copy(ins[k], iv[i], isem.at[i]) for i, k in enumerate(order)}
+    val = {k: iv[i] for i, k in enumerate(order)}
+    for k in order: src[k].start()
+    done = []
+    def copy(a, b, i):
+        c = pltpu.make_async_copy(a, b, osem.at[i]); c.start(); done.append(c)
+    put = {k: i for i, k in enumerate((0, 4, 5, 6, 7, 8, 9, 10, 11, 12, 13, 14, 15))}
+    def out(k): copy(ov[put[k]], outs[k], k)
+    at = lambda k: ov[put[k]]
+    for w, q, m, v, ks in ((8, 4, 9, 10, (7, 8, 12, 15)), (5, 3, 6, 7, (5, 6, 11, 14))):
+        for k in (w, q, m, v): src[k].wait()
+        new = update(val[w][...], val[q][...], val[m][...], val[v][...], weight_decay, at(ks[0]), at(ks[1]), at(ks[2]))
+        at(ks[3])[...] = new.astype(bf16)
+        for k in ks: out(k)
+        copy(val[q], outs[q - 1], q - 1)
+    src[1].wait()
+    copy(val[1], outs[1], 1)
+    for k in (11, 12, 13, 2): src[k].wait()
+    q = val[2][0:2, 0:gl]
+    w = val[11][...]
+    at(4)[...] = q
+    at(13)[...] = update(w, q, val[12][...], val[13][...], 0.0, at(9), at(10), at(13)) - w
+    for k in (4, 9, 10, 13): out(k)
+    src[0].wait()
+    def pm(j): at(0)[j] = val[0][slot[j]]
     loop(0, N, pm)
-    iout[...] = io[...]
-    ago[...] = ag[...]
-    fgo[...] = fg[...]
-    q = gs[0:2, 0:gl]
-    ggo[...] = q
-    ac[...] = update(am[...], ag[...], amm[...], amv[...], weight_decay, amo, avo, awo).astype(bf16)
-    fc[...] = update(fm[...], fg[...], fmm[...], fmv[...], weight_decay, fmo, fvo, fwo).astype(bf16)
-    w = gm[...]
-    gup[...] = update(w, q, gmm[...], gmv[...], 0.0, gmo, gvo, gup) - w
+    out(0)
+    for c in done: c.wait()
 
 
 def last_call(slot, oo, io, gs, ag, fg, am, amm, amv, fm, fmm, fmv, gm, gmm, gmv):
-    V = pl.BlockSpec(memory_space=pltpu.VMEM); SM = pl.BlockSpec(memory_space=pltpu.SMEM)
+    A = pl.BlockSpec(memory_space=pltpu.HBM); SM = pl.BlockSpec(memory_space=pltpu.SMEM)
     sd = lambda a, dt=None: jax.ShapeDtypeStruct(a.shape, dt or a.dtype)
-    return pl.pallas_call(last_kernel, in_specs=[SM] + [V] * 14, out_specs=(V,) * 16,
-        out_shape=(sd(oo), sd(io), sd(am), sd(fm), sd(gm), sd(am), sd(am), sd(fm), sd(fm), sd(gm), sd(gm), sd(am), sd(fm), sd(gm), sd(am, bf16), sd(fm, bf16)),
-        compiler_params=pltpu.CompilerParams(vmem_limit_bytes=48 * 2**20))(slot, oo, io, gs, ag, fg, am, amm, amv, fm, fmm, fmv, gm, gmm, gmv)
+    args = (oo, io, gs, ag, fg, am, amm, amv, fm, fmm, fmv, gm, gmm, gmv)
+    res = (sd(oo), sd(io), sd(am), sd(fm), sd(gm), sd(am), sd(am), sd(fm), sd(fm), sd(gm), sd(gm), sd(am), sd(fm), sd(gm), sd(am, bf16), sd(fm, bf16))
+    vm = lambda a: pltpu.VMEM(a.shape, a.dtype)
+    return pl.pallas_call(last_kernel, in_specs=[SM] + [A] * 14, out_specs=(A,) * 16, out_shape=res,
+        scratch_shapes=[vm(args[k]) for k in (8, 9, 10, 4, 5, 6, 7, 3, 1, 11, 12, 13, 2, 0)] + [vm(res[k]) for k in (0, 4, 5, 6, 7, 8, 9, 10, 11, 12, 13, 14, 15)]
+                       + [pltpu.SemaphoreType.DMA((14,)), pltpu.SemaphoreType.DMA((16,))],
+        compiler_params=pltpu.CompilerParams(vmem_limit_bytes=64 * 2**20))(slot, *args)
 
 
 def local_one(tokens, cotangent, lengths, device_sequence, slot_device, attention_master, feedforward_master, gains_master,
@@ -889,7 +1020,10 @@
     slot_of_sequence = jnp.sum(jnp.where(slot_sequence[:, None] == counter[None, :], counter[:, None], 0), axis=0)
     tr = lambda a: a.transpose(1, 0, 2)
     C, S = tables(tokens.shape[1] * N)
-    oo, io, gs, ag, fg = all_call(slot_of_sequence, lengths, tokens, cotangent, gains_master, attention_master, tr(feedforward_master), jnp.asarray(C), jnp.asarray(S))
+    width = tokens.shape[2]
+    oo, io, gs, ag, fg = all_call(slot_of_sequence, lengths, tokens, cotangent, gains_master, attention_master,
+                                  tr(feedforward_master).reshape(-1, width), jnp.asarray(C), jnp.asarray(S))
+    fg = fg.reshape(3, -1, width)
     r = list(last_call(slot_sequence, oo, io, gs, ag, fg, attention_master, attention_mean, attention_square,
                        tr(feedforward_master), tr(feedforward_mean), tr(feedforward_square), gains_master, gains_mean, gains_square))
     for i in (3, 7, 8, 12, 15): r[i] = tr(r[i])

time: 254 us -> 203 us (0.80)
  Pallas kernels: 238 us -> 199 us
  local copies, waits for them, and re-layouts: 12.2 us -> 1.18 us
    pallas_call x1, Pallas kernels: 234 us -> 193 us  [all_call(): pl.pallas_call(functools.partial(all_kernel, nf, nd), out_shape=(sd(tok.s...]
    unnamed x36 -> x6, local copies, waits for them, and re-layouts: 12.2 us -> 1.18 us
where the time goes in v3:
time: 203 us; the launch traced here: 201 us
  Pallas kernels  199 us (98%)
    pallas_call x1, Pallas kernels, all_call(): pl.pallas_call(functools.partial(all_kernel, nf, nd), out_shape=(sd(tok.s...  193 us
    pallas_call x1, Pallas kernels, last_call(): pl.pallas_call(last_kernel, in_specs=[SM] + [A] * 14, out_specs=(A,) * 16...  5.29 us

profile of v3, /device:TPU:8, one launch (start us, length us, event | category | flops | bytes accessed | tf_op | source)
XLA Modules:
  0.0 201.4 jit_solution(15892367710363290020)
XLA Ops:
  0.6 0.0 copy-start.1
  0.7 0.0 copy-start.2
  0.7 0.6 copy-done.1
  1.3 0.0 copy-done.2
  1.3 0.2 select_reduce_fusion.1.slot
  1.5 0.0 copy-start
  1.5 0.5 copy-done
  2.0 0.6 select_reduce_fusion.perm
  2.6 193.4 %shard_map.279 = (bf16[32,16,768]{2,1,0:T(8,128)(2,1)}, bf16[32,16,768]{2,1,0:T(8,128)(2,1)}, f32[8,128]{1,0:T(8,128)}, f32[96,768]{1,0:T(8,128)}, f32[192,768]{1,0:T(8,128)}) custom-call(s32[32]{0:T(128)} %select_reduce_fusion.perm, s32[32]{0:T(128)} %lens.1, bf16[32,16,768]{2,1,0:T(8,128)(2,1)} %tok.1, bf16[32,16,768]{2,1,0:T(8,128)(2,1)} %cot0.1, ...), custom_call_target="tpu_custom_call" | custom-call | tf_op jit(solution)/shard_map/pallas_call | solution.py:946
  196.0 5.3 %shard_map.280 = (bf16[32,16,768]{2,1,0:T(8,128)(2,1)}, bf16[32,16,768]{2,1,0:T(8,128)(2,1)}, f32[96,768]{1,0:T(8,128)}, f32[3,64,768]{2,1,0:T(8,128)}, f32[2,24...) custom-call(s32[32]{0:T(128)} %copy-done, ...), custom_call_target="tpu_custom_call" | custom-call | tf_op jit(solution)/shard_map/pallas_call | solution.py:1009
Async XLA Ops:
  0.6 0.7 copy-start.1
  0.7 0.7 copy-start.2
  1.5 0.5 copy-start

commit v4 on v3

--- a/solution.py
+++ b/solution.py
@@ -538,6 +538,14 @@
         return (y * 2 + x) * 2 + cc
 
 
+def near(t, i):
+    r = 0
+    for z in range(t.Z):
+        by = sorted(range(t.Z), key=lambda q: (abs(q - z), q))
+        for k in range(t.Z): r = r + jnp.where((t.z == z) & (i == k), by[k], 0)
+    return r
+
+
 class Gather2:
     def __init__(s, t, at, ssem, zsem, rsem): s.t, s.at, s.ssem, s.zsem, s.rsem = t, at, ssem, zsem, rsem
     def send(s, z, g, dev):
@@ -582,19 +590,21 @@
 
 
 class Scatter3:
-    def __init__(s, t, at, ld, rc, r1, r2, rz, ss, rcs, r1s, r2s, rzs, zss):
+    def __init__(s, t, at, ld, rc, r1, r2, rz, ss, rcs, r1s, r2s, rzs, zss, far=True):
+        s.far = far
         s.t, s.at, s.ld, s.rc, s.r1, s.r2, s.rz, s.ss, s.rcs, s.r1s, s.r2s, s.rzs, s.zss = t, at, ld, rc, r1, r2, rz, ss, rcs, r1s, r2s, rzs, zss
         s.Z = Z = t.Z
-        s.order = [sorted(range(Z), key=lambda q: (-abs(q - z), (q > z) == (z < Z // 2))) for z in range(Z)]
+        far_order = [sorted(range(Z), key=lambda q: (-abs(q - z), (q > z) == (z < Z // 2))) for z in range(Z)]
+        s.order = far_order if far else [sorted(range(Z), key=lambda q: (abs(q - z), q)) for z in range(Z)]
     def zof(s, i):
         r = 0
         for z in range(s.Z): r = r + jnp.where(s.t.z == z, s.order[z][i], 0)
         return r
-    def start(s, gi):
-        t = s.t; Z = s.Z; g = t.g8(gi, t.cb)
-        for i in range(Z):
-            z = s.zof(i); j = (3 - gi) * Z + z
-            rcopy(s.at(z, g), s.rc.at[j], s.ss.at[0], s.rcs.at[j], t.sib).start()
+    def start(s, z):
+        t = s.t
+        for gi in range(4):
+            j = (3 - gi) * s.Z + z
+            rcopy(s.at(z, t.g8(gi, t.cb)), s.rc.at[j], s.ss.at[0], s.rcs.at[j], t.sib).start()
     def chip(s, z, gs):
         t = s.t; Z = s.Z
         for gi in gs:
@@ -631,11 +641,28 @@
         for i in ii: s.chip(s.zof(i), (3, 2, 1, 0))
     def F(s, *ii):
         for i in ii: s.first(s.zof(i))
+    def straight(s, z):
+        t = s.t
+        return rcopy(s.r2.at[z], s.rz.at[t.z], s.zss.at[z], s.rzs.at[t.z], t.dev(z, t.y, t.x, t.c))
+    def D(s, *ii):
+        for i in ii:
+            z = s.zof(i)
+            s.second(z)
+            @pl.when(z != s.t.z)
+            def _(): s.straight(z).start()
     def S(s, *ii):
         for i in ii: s.second(s.zof(i)); s.line(s.zof(i))
     def total(s):
         t = s.t; Z = s.Z
         tot = s.r2[t.z].astype(f32)
+        if not s.far:
+            for q in range(Z):
+                @pl.when(t.z != q)
+                def _(): wait_bytes(s.rz.at[q], s.rzs.at[q])
+                @pl.when(t.z == q)
+                def _(): s.rz[q] = jnp.zeros(s.rz.shape[1:], bf16)
+                tot = tot + s.rz[q].astype(f32)
+            return tot
         below = jnp.where(t.z > 0, 1.0, 0.0); above = jnp.where(t.z < Z - 1, 1.0, 0.0)
         @pl.when(t.z > 0)
         def _(): wait_bytes(s.rz.at[t.z], s.rzs.at[t.z])
@@ -650,6 +677,10 @@
         t = s.t; Z = s.Z
         wait_bytes(s.rc, s.ss.at[0]); wait_bytes(s.r1, s.ss.at[1]); wait_bytes(s.r2, s.ss.at[2])
         def f(z):
+            if not s.far:
+                @pl.when(z != t.z)
+                def _(): s.straight(z).wait_send()
+                return
             for side in (-1, 1):
                 @pl.when((z - t.z) * side > 0)
                 def _(): s.hop(z, side).wait_send()
@@ -788,11 +819,11 @@
     blk_at = lambda ref: (lambda z, g: ref.at[z * 8 + g])
     most = lambda ref: ref.at[pl.ds(0, L - pos)]
     f0 = b2.at[pl.ds(0, ra)], dn2.at[pl.ds(0, 3 * R)]
-    near = [pltpu.make_async_copy(a, d, ls.at[5 + i]) for i, (a, d) in enumerate(((am, f0[0]), (fm, f0[1]), (cot0, o), (cos_ref, cs), (sin_ref, sn)))]
-    for c in near: c.start()
-    near[0].wait()
+    near_w = [pltpu.make_async_copy(a, d, ls.at[5 + i]) for i, (a, d) in enumerate(((am, f0[0]), (fm, f0[1]), (cot0, o), (cos_ref, cs), (sin_ref, sn)))]
+    for c in near_w: c.start()
+    near_w[0].wait()
     wa[pl.ds(pl.multiple_of(t.me * ra, ra), ra), :] = f0[0][...].astype(bf16)
-    near[1].wait()
+    near_w[1].wait()
     wf[t.me] = f0[1][...].astype(bf16).reshape(3, R, 768)
     gt[...] = jnp.zeros_like(gt)
     gt[0:2, 0:gl] = gm[...].astype(bf16).astype(f32)
@@ -811,13 +842,15 @@
     tk.more(8)
     takes(A, 0, 3, (tk, 3))
     F.start()
-    near[2].wait()
+    near_w[2].wait()
     def pm(i): cst[pl.ds(pl.multiple_of(i * pos, pos), pos), :] = o[perm[i]]
     loop(0, N, pm)
     ct.start()
     def gs(k): rcopy(gt, gg.at[t.me], ss.at[2], rs.at[2], t.flat(lax.rem(t.me + k, N))).start()
     loop(1, N, gs)
-    takes(A, 3, 15, (tk, 3))
+    takes(A, 3, 8, (tk, 3))
+    takes(A, 8, 15, (tk, 8), (ct, 4))
+
     tk.more(N)
     for gi in range(4): A.take_sib(gi)
     tk.wait_recv()
@@ -827,22 +860,27 @@
         wide = jnp.concatenate([gg[d], jnp.zeros((8, 640), f32)], 1)
         tot = tot + (pltpu.roll(wide, d * gl, 1) if d else wide)
     gains[...] = tot
-    takes(F, 0, 2, (ct, 3))
+    takes(F, 0, 2, (ct, 8))
+
     phase_norm1(xg, gains, n1)
-    takes(F, 2, 4, (ct, 3))
-    near[3].wait(); near[4].wait()
+    takes(F, 2, 3)
+
+    near_w[3].wait(); near_w[4].wait()
     phase_qkv(n1, wa, cs, sn, qkv)
-    takes(F, 4, 6, (ct, 4))
+    takes(F, 3, 5)
     def fwd(i):
         attn_fwd2(qkv, ps, o, i, i + 1)
     loop(0, 2, fwd)
-    takes(F, 6, 8, (ct, 4))
+    takes(F, 5, 6)
     loop(2, 4, fwd)
-    takes(F, 8, 10, (ct, 4))
+    takes(F, 6, 7)
     loop(4, 6, fwd)
+    takes(F, 7, 8)
+
     ct.more(N)
     wo_norm2(o, wa, xg, gains, hs, n2)
-    takes(F, 10, 11)
+    takes(F, 8, 9)
+
     ct.wait_recv()
     n = lens[t.me]
     def mask(r, of):
@@ -850,18 +888,22 @@
         cg[r, :] = jnp.where(row < n, cg[r, :].astype(f32), 0.0).astype(bf16)
     rows_loop(L, mask)
     SA = Scatter3(t, row_at(gatt), lambda z, g: gatt[pl.ds(pl.multiple_of((z * 8 + g) * ra, ra), ra), :], arc, ar1, ar2, arz, ass, acs, a1s, a2s, azs, azq)
-    SF = Scatter3(t, blk_at(gff), lambda z, g: gff[z * 8 + g], frc, fr1, fr2, frz, fss, fcs, f1s, f2s, fzs, fzq)
+    SF = Scatter3(t, blk_at(gff), lambda z, g: gff[z * 8 + g], frc, fr1, fr2, frz, fss, fcs, f1s, f2s, fzs, fzq, far=False)
     def tile(i):
-        gi = i // 2
-        par = lax.rem(lax.rem(i, 2) + i // 6, 2)
+        z = near(t, i // 2)
+        par = lax.rem(i, 2)
         cc = t.c + par * (1 - 2 * t.c)
-        g = t.g8(gi, cc)
-        for k, lo, hi in ((1, 11, 12), (2, 12, 13), (3, 13, 14), (4, 14, 15)):
+        slots = [z * 8 + q * 2 + cc for q in range(4)]
+        for k, lo, hi in ((1, 9, 11), (2, 11, 12), (3, 12, 13), (4, 13, 14), (6, 14, 15)):
             @pl.when(i == k)
             def _(): takes(F, lo, hi)
+        for k in range(Z - 1):
+            @pl.when(i == 2 * k + 3)
+            def _(): SF.C(k)
         @pl.when(par == 1)
-        def _(): F.take_sib(gi)
-        wg, wu, wd = (jnp.concatenate([wf[z * 8 + g, j] for z in range(Z)], 0) for j in range(3))
+        def _():
+            for q in range(4): F.wait(z, q * 2 + cc)
+        wg, wu, wd = (jnp.concatenate([wf[sl, j] for sl in slots], 0) for j in range(3))
         nv = n2[...]
         ga = dot_nt(nv, wg); u = dot_nt(nv, wu)
         da = dot_nt(cg[...], wd)
@@ -880,31 +922,32 @@
             b2[...] += bb; dn2[...] += dn
         for j, (lhs, rhs) in enumerate(((dg, nv), (du, nv), (a, cg[...]))):
             w = dot_tn(lhs, rhs).astype(bf16)
-            for z in range(Z): gff[z * 8 + g, j] = w[z * R:(z + 1) * R]
+            for q, sl in enumerate(slots): gff[sl, j] = w[q * R:(q + 1) * R]
         @pl.when(par == 1)
-        def _(): SF.start(gi)
+        def _(): SF.start(z)
     loop(0, 8, tile)
     ox = Exchange(t, rows_of(cg, pos), lambda d: oo.at[d], most(cg), oo.at[pl.ds(0, N - 1)], ss.at[5], rs.at[3], ls.at[3])
     ix = Exchange(t, rows_of(n1, pos), lambda d: io.at[d], most(n1), io.at[pl.ds(0, N - 1)], ss.at[6], rs.at[4], ls.at[4])
-    SF.C(0, 1)
     mid2(n, cg, hs, b2, dn2, gains, n2, ggb)
+    SF.C(3)
     ox.start(); ox.more(8)
     ct.wait_send()
     wo_back2(n2, o, wa, cst, gatt)
-    ox.more(8)
+    SF.F(0, 1); SF.D(0); ox.more(8)
     def back(i):
         attn_bwd2(qkv, ps, cst, cs, sn, i, i + 1)
-    loop(0, 1, back)
-    SF.F(0); SF.C(2); ox.more(8)
-    loop(1, 4, back)
-    SF.F(1); SF.S(0); SF.C(3); ox.more(N)
+    loop(0, 2, back)
+    ox.more(8)
+    loop(2, 4, back)
+    SF.F(2); SF.D(1); ox.more(N)
     loop(4, 6, back)
     phase_wqkv_grad(qkv, n1, gatt)
-    for gi in (3, 2, 1, 0): SA.start(gi)
-    SF.F(2); SF.S(1)
+    for i in range(Z): SA.start(SA.zof(i))
+    SF.F(3); SF.D(2)
+    SA.C(0, 1)
     phase_dn1(qkv, wa, xg, gains, hs, n1, ggb)
-    SA.C(0, 1)
     ix.start(); ix.more(8)
+    SF.D(3)
     for d in range(N):
         v = ggb[...]
         gb[d] = (pltpu.roll(v, 768 - d * gl, 1) if d else v)[:, 0:128]
@@ -913,9 +956,7 @@
         d = lax.rem(t.me + k, N)
         rcopy(gb.at[d], ggr.at[t.me], ss.at[7], rs.at[5], t.flat(d)).start()
     loop(1, N, gsend)
-    SF.F(3); SF.S(2)
     SA.F(0); SA.C(2); ix.more(8)
-    SF.S(3)
     SA.F(1); SA.S(0); SA.C(3); ix.more(N)
     SA.F(2); SA.S(1)
     f0[1][...] = SF.total().reshape(3 * R, 768)

time: 203 us -> 199 us (0.980)
  Pallas kernels: 199 us -> 195 us
    pallas_call x1, Pallas kernels: 193 us -> 190 us  [all_call(): pl.pallas_call(functools.partial(all_kernel, nf, nd), out_shape=(sd(tok.s...]
where the time goes in v4:
time: 199 us; the launch traced here: 198 us
  Pallas kernels  195 us (98%)
    pallas_call x1, Pallas kernels, all_call(): pl.pallas_call(functools.partial(all_kernel, nf, nd), out_shape=(sd(tok.s...  190 us
    pallas_call x1, Pallas kernels, last_call(): pl.pallas_call(last_kernel, in_specs=[SM] + [A] * 14, out_specs=(A,) * 16...  5.29 us

profile of v4, /device:TPU:8, one launch (start us, length us, event | category | flops | bytes accessed | tf_op | source)
XLA Modules:
  0.0 197.9 jit_solution(18372354361663036930)
XLA Ops:
  0.6 0.0 copy-start.1
  0.7 0.0 copy-start.2
  0.7 0.6 copy-done.1
  1.3 0.0 copy-done.2
  1.3 0.2 select_reduce_fusion.1.slot
  1.5 0.0 copy-start
  1.5 0.5 copy-done
  2.0 0.6 select_reduce_fusion.perm
  2.6 189.8 %shard_map.279 = (bf16[32,16,768]{2,1,0:T(8,128)(2,1)}, bf16[32,16,768]{2,1,0:T(8,128)(2,1)}, f32[8,128]{1,0:T(8,128)}, f32[96,768]{1,0:T(8,128)}, f32[192,768]{1,0:T(8,128)}) custom-call(s32[32]{0:T(128)} %select_reduce_fusion.perm, s32[32]{0:T(128)} %lens.1, bf16[32,16,768]{2,1,0:T(8,128)(2,1)} %tok.1, bf16[32,16,768]{2,1,0:T(8,128)(2,1)} %cot0.1, ...), custom_call_target="tpu_custom_call" | custom-call | tf_op jit(solution)/shard_map/pallas_call | solution.py:987
  192.4 5.3 %shard_map.280 = (bf16[32,16,768]{2,1,0:T(8,128)(2,1)}, bf16[32,16,768]{2,1,0:T(8,128)(2,1)}, f32[96,768]{1,0:T(8,128)}, f32[3,64,768]{2,1,0:T(8,128)}, f32[2,24...) custom-call(s32[32]{0:T(128)} %copy-done, ...), custom_call_target="tpu_custom_call" | custom-call | tf_op jit(solution)/shard_map/pallas_call | solution.py:1050
Async XLA Ops:
  0.6 0.7 copy-start.1
  0.7 0.7 copy-start.2
  1.5 0.5 copy-start

commit v5 on v4

--- a/solution.py
+++ b/solution.py
@@ -849,7 +849,12 @@
     def gs(k): rcopy(gt, gg.at[t.me], ss.at[2], rs.at[2], t.flat(lax.rem(t.me + k, N))).start()
     loop(1, N, gs)
     takes(A, 3, 8, (tk, 3))
-    takes(A, 8, 15, (tk, 8), (ct, 4))
+    takes(F, 0, 1)
+    takes(A, 8, 10, (tk, 8), (ct, 5))
+    takes(F, 1, 2)
+    takes(A, 10, 13, (ct, 5))
+    takes(F, 2, 3)
+    takes(A, 13, 15, (ct, 5))
 
     tk.more(N)
     for gi in range(4): A.take_sib(gi)
@@ -860,14 +865,14 @@
         wide = jnp.concatenate([gg[d], jnp.zeros((8, 640), f32)], 1)
         tot = tot + (pltpu.roll(wide, d * gl, 1) if d else wide)
     gains[...] = tot
-    takes(F, 0, 2, (ct, 8))
+    ct.more(N)
 
     phase_norm1(xg, gains, n1)
-    takes(F, 2, 3)
+    takes(F, 3, 4)
 
     near_w[3].wait(); near_w[4].wait()
     phase_qkv(n1, wa, cs, sn, qkv)
-    takes(F, 3, 5)
+    takes(F, 4, 5)
     def fwd(i):
         attn_fwd2(qkv, ps, o, i, i + 1)
     loop(0, 2, fwd)

time: 199 us -> 194 us (0.975)
  Pallas kernels: 195 us -> 190 us
    pallas_call x1, Pallas kernels: 190 us -> 185 us  [all_call(): pl.pallas_call(functools.partial(all_kernel, nf, nd), out_shape=(sd(tok.s...]
where the time goes in v5:
time: 194 us; the launch traced here: 193 us
  Pallas kernels  190 us (98%)
    pallas_call x1, Pallas kernels, all_call(): pl.pallas_call(functools.partial(all_kernel, nf, nd), out_shape=(sd(tok.s...  185 us
    pallas_call x1, Pallas kernels, last_call(): pl.pallas_call(last_kernel, in_specs=[SM] + [A] * 14, out_specs=(A,) * 16...  5.29 us

profile of v5, /device:TPU:8, one launch (start us, length us, event | category | flops | bytes accessed | tf_op | source)
XLA Modules:
  0.0 193.2 jit_solution(12490015576286944838)
XLA Ops:
  0.6 0.0 copy-start.1
  0.7 0.0 copy-start.2
  0.7 0.6 copy-done.1
  1.3 0.0 copy-done.2
  1.3 0.2 select_reduce_fusion.1.slot
  1.5 0.0 copy-start
  1.5 0.5 copy-done
  2.0 0.6 select_reduce_fusion.perm
  2.6 185.1 %shard_map.279 = (bf16[32,16,768]{2,1,0:T(8,128)(2,1)}, bf16[32,16,768]{2,1,0:T(8,128)(2,1)}, f32[8,128]{1,0:T(8,128)}, f32[96,768]{1,0:T(8,128)}, f32[192,768]{1,0:T(8,128)}) custom-call(s32[32]{0:T(128)} %select_reduce_fusion.perm, s32[32]{0:T(128)} %lens.1, bf16[32,16,768]{2,1,0:T(8,128)(2,1)} %tok.1, bf16[32,16,768]{2,1,0:T(8,128)(2,1)} %cot0.1, ...), custom_call_target="tpu_custom_call" | custom-call | tf_op jit(solution)/shard_map/pallas_call | solution.py:992
  187.8 5.3 %shard_map.280 = (bf16[32,16,768]{2,1,0:T(8,128)(2,1)}, bf16[32,16,768]{2,1,0:T(8,128)(2,1)}, f32[96,768]{1,0:T(8,128)}, f32[3,64,768]{2,1,0:T(8,128)}, f32[2,24...) custom-call(s32[32]{0:T(128)} %copy-done, ...), custom_call_target="tpu_custom_call" | custom-call | tf_op jit(solution)/shard_map/pallas_call | solution.py:1055
Async XLA Ops:
  0.6 0.7 copy-start.1
  0.7 0.7 copy-start.2
  1.5 0.5 copy-start
